TPU v7x, 128 devices: a whole 4x4x4 slice. The times are simulated.
128 devices in a mesh: sec: 2 (over y_lo), dev: 64 (over x, y_hi, z, core).
Axes of the slice: x: 4, y: 4 (y_hi: 2, y_lo: 2; y = y_hi * 2 + y_lo), z: 4, core: 2. Of those that a mesh axis runs over, the one named last changes fastest.
Arguments:
- hidden_in: bfloat16 [4096, 4096], P(('sec', 'dev')), may hold values from -6 to 6
- routes: int32 [4096, 8], P(('sec', 'dev')), may hold values from 0 to 63, all different within a row; in each aligned block of 32 rows (0 to 31, 32 to 63, ...) at most 8 rows name the same one
- scores: float32 [4096, 8], P(('sec', 'dev')), may hold values from 0.05 to 1
- w_gate: bfloat16 [64, 4096, 1536], P('dev', None, 'sec'), may hold values from -0.09375 to 0.09375
- w_up: bfloat16 [64, 4096, 1536], P('dev', None, 'sec'), may hold values from -0.09375 to 0.09375
- w_down: bfloat16 [64, 1536, 4096], P('dev', 'sec'), may hold values from -0.15625 to 0.15625
Outputs:
- mixed: bfloat16 [4096, 4096], P(('sec', 'dev'))
Inputs may be any that keep to these rules, and one draw needn't show every extreme that they name: `routes`: each row names 8 different experts; among the rows of one device no expert is named by more than 8 rows, and in every draw some expert is named by exactly 8 rows of some device.
All inputs are finite; a program needn't handle non-finite values.
Results may differ from a plain program's by a relative error of at most 0.017.
Values may be sent and summed in bfloat16 or wider, within the bound.
A program may use at most 128 MiB of HBM per device.

v0:
```python
import jax
import jax.numpy as jnp
from jax import lax
from jax.sharding import PartitionSpec as P


def on_device(hidden_in, routes, scores, w_gate, w_up, w_down):
    rows_dev, model_width = hidden_in.shape
    top_k = routes.shape[1]
    experts = lax.axis_size("dev")
    slots_dev = 2 * rows_dev * top_k // experts
    slot_rows = experts * slots_dev
    values = hidden_in.astype(jnp.float32)
    normed = (values * lax.rsqrt(jnp.mean(values * values, -1, keepdims=True) + 1e-06)).astype(
        jnp.bfloat16
    )
    shares = scores / jnp.sum(scores, -1, keepdims=True)
    chosen = routes.reshape(-1)
    onehot = (chosen[:, None] == jnp.arange(experts, dtype=jnp.int32)[None, :]).astype(jnp.int32)
    before = jnp.cumsum(onehot, 0) - onehot
    position = jnp.sum(before * onehot, 1)
    target = (chosen * slots_dev + position).reshape(rows_dev, top_k)
    places = jnp.arange(slot_rows, dtype=jnp.int32)
    picker = jnp.any(target[None, :, :] == places[:, None, None], -1).astype(jnp.bfloat16)
    outgoing = jnp.dot(picker, normed, preferred_element_type=jnp.float32).astype(jnp.bfloat16)
    outgoing = outgoing.reshape(experts, slots_dev, model_width)
    arrived = lax.all_to_all(outgoing, "dev", split_axis=0, concat_axis=0, tiled=True).reshape(
        slot_rows, model_width
    )
    paired = lax.all_gather(arrived, "sec", axis=0, tiled=True)
    gate_part = jnp.dot(paired, w_gate[0], preferred_element_type=jnp.float32)
    up_part = jnp.dot(paired, w_up[0], preferred_element_type=jnp.float32)
    hidden_part = (jax.nn.silu(gate_part) * up_part).astype(jnp.bfloat16)
    result = lax.psum_scatter(
        jnp.dot(hidden_part, w_down[0], preferred_element_type=jnp.float32).astype(jnp.bfloat16),
        "sec",
        scatter_dimension=0,
        tiled=True,
    )
    expert_out = result.reshape(experts, slots_dev, model_width)
    returned = lax.all_to_all(expert_out, "dev", split_axis=0, concat_axis=0, tiled=True).reshape(
        slot_rows, model_width
    )
    picked = jnp.take(returned, target.reshape(-1), axis=0).reshape(rows_dev, top_k, model_width)
    combined = jnp.einsum("rk,rkd->rd", shares, picked.astype(jnp.float32))
    return combined.astype(jnp.bfloat16)


def solution(mesh):
    placed = (
        P(("sec", "dev"), None),
        P(("sec", "dev"), None),
        P(("sec", "dev"), None),
        P("dev", None, "sec"),
        P("dev", None, "sec"),
        P("dev", "sec", None),
    )
    return jax.shard_map(
        on_device, mesh=mesh, in_specs=placed, out_specs=P(("sec", "dev"), None), check_vma=False
    )
```

profile of v0, /device:TPU:1, one launch (start us, length us, event | category | flops | bytes accessed | tf_op | source)
XLA Modules:
  0.0 391.9 jit_solution(4126649069712633075)
XLA Ops:
  6.5 0.0 all-gather.2.cloned.1.call-start
  6.5 0.8 copy.13
  7.3 0.1 eq.39
  7.4 0.1 reshape.89
  7.5 0.6 reduce-window.6
  8.1 0.2 slice_reduce_fusion
  8.3 0.1 fusion.18
  8.4 0.1 reduce_sum.33
  8.6 0.2 fusion.13
  8.8 1.1 fusion.11
  9.9 2.3 fusion.5
  12.2 65.3 %all_to_all.10 = bf16[64,8,4096]{2,1,0:T(8,128)(2,1)} all-to-all(bf16[64,8,4096]{2,1,0:T(8,128)(2,1)S(1)} %fusion.5), channel_id=1, replica_groups=mesh['sec'=2,'dev'=64] {'dev'}, dimensions={0} | all-to-all | bytes 8388608 | tf_op jit(solution)/shard_map/all_to_all | solution.py:27
  77.5 0.0 all-gather.2.cloned.1.call-update
  77.6 0.2 reduce-scatter.2.cloned.1.call-start
  77.8 103.0 %all-gather.2.cloned.1.call-done = bf16[1024,4096]{1,0:T(8,128)(2,1)} async-done(((bf16[512,4096]{1,0:T(8,128)(2,1)}), bf16[1024,4096]{1,0:T(8,128)(2,1)}) %all-gather.2.cloned.1.call-update) | async-done | bytes 8388624 | tf_op jit(solution)/shard_map/all_gather | solution.py:30
  180.8 11.0 %fusion.1 = f32[1024,768]{1,0:T(8,128)S(1)} fusion(bf16[1024,4096]{1,0:T(8,128)(2,1)} %all-gather.2.cloned.1.call-done, bf16[1,4096,768]{2,1,0:T(8,128)(2,1)} %param.10), kind=kOutput, calls=%fused_computation.3 | convolution fusion | flops 6442450944 | bytes 17825792 | tf_op jit(solution)/shard_map/dot_general | solution.py:32
  191.8 0.0 copy-done.1
  191.8 0.0 slice-start.1
  191.8 9.9 %multiply_convert_fusion = bf16[1024,768]{1,0:T(8,128)(2,1)S(1)} fusion(f32[1024,768]{1,0:T(8,128)S(1)} %fusion.1, bf16[1024,4096]{1,0:T(8,128)(2,1)S(1)} %copy-done.1, bf16[1,4096,768]{2,1,0:T(8,128)(2,1)} %param.9), kind=kOutput, calls=%fused_computation.9 | convolution fusion | flops 6447169536 | bytes 19398656 | tf_op jit(solution)/shard_map/dot_general | solution.py:31
  201.7 0.0 slice-done
  201.7 0.0 slice-done.1
  201.8 8.8 %convolution_convert_fusion = bf16[1024,4096]{1,0:T(8,128)(2,1)} fusion(bf16[1024,768]{1,0:T(8,128)(2,1)S(1)} %multiply_convert_fusion, bf16[1,768,4096]{2,1,0:T(8,128)(2,1)S(1)} %bitcast.55), kind=kOutput, calls=%fused_computation.1 | convolution fusion | flops 6446645248 | bytes 16252928 | tf_op jit(solution)/shard_map/dot_general | solution.py:35
  210.6 0.0 reduce-scatter.2.cloned.1.call-update
  210.6 102.9 %reduce-scatter.2.cloned.1.call-done = bf16[512,4096]{1,0:T(8,128)(2,1)} async-done(((bf16[1024,4096]{1,0:T(8,128)(2,1)}), bf16[512,4096]{1,0:T(8,128)(2,1)}) %reduce-scatter.2.cloned.1.call-update) | async-done | bytes 4194320 | tf_op jit(solution)/shard_map/reduce_scatter | solution.py:34
  313.5 10.6 %all-to-all-start.1 = ((bf16[64,8,4096]{2,1,0:T(8,128)(2,1)}), bf16[64,8,4096]{2,1,0:T(8,128)(2,1)}, u32[]{:S(2)}, u32[]{:S(2)}) async-start(bf16[64,8,4096]{2,1,0:T(8,128)(2,1)} %bitcast.51), calls=%async_computation.2 | async-start | bytes 8388608 | tf_op jit(solution)/shard_map/all_to_all | solution.py:41
  324.1 0.1 mul.50
  324.2 0.0 copy-done
  324.2 0.1 copy.17
  324.4 52.3 %all-to-all-done.1 = bf16[64,8,4096]{2,1,0:T(8,128)(2,1)} async-done(((bf16[64,8,4096]{2,1,0:T(8,128)(2,1)}), bf16[64,8,4096]{2,1,0:T(8,128)(2,1)}, u32[]{:S(2)}, u32[]{:S(2)}) %all-to-all-start.1) | async-done | bytes 4194336 | tf_op jit(solution)/shard_map/all_to_all | solution.py:41
  376.7 6.6 %gather_fusion = bf16[256,4096]{1,0:T(8,128)(2,1)S(1)} fusion(bf16[512,4096]{1,0:T(8,128)(2,1)} %bitcast.8, s32[1024]{0:T(1024)S(1)} %pad_clamp_fusion), kind=kCustom, calls=%fused_computation | custom fusion | bytes 4195328 | tf_op jit(solution)/shard_map/jit(_take)/gather | solution.py:44
  383.3 0.8 fusion.8
  384.1 1.0 copy.22
  (14 shorter events, 0.1 us)
Async XLA Ops:
  6.5 174.2 %all-gather.2.cloned.1.call-start = ((), (), s32[]{:S(2)}) async-start(), calls=%async_computation.3 | async-start | bytes 12582912 | tf_op jit(solution)/shard_map/all_gather | solution.py:30
  77.6 236.0 %reduce-scatter.2.cloned.1.call-start = ((), (), s32[]{:S(2)}) async-start(), calls=%async_computation.4 | async-start | bytes 12582912 | tf_op jit(solution)/shard_map/reduce_scatter | solution.py:34
  180.8 11.0 %copy-start.1 = (bf16[1024,4096]{1,0:T(8,128)(2,1)S(1)}, bf16[1024,4096]{1,0:T(8,128)(2,1)}, u32[]{:S(2)}) copy-start(bf16[1024,4096]{1,0:T(8,128)(2,1)} %all-gather.2.cloned.1.call-done) | copy-start | bytes 25165828
  180.8 21.0 %slice-start = ((s8[6291456]{0:T(1024)(128)(4,1)}), s8[4194304]{0:T(1024)(128)(4,1)S(1)}, s32[]{:S(2)}) async-start(s8[6291456]{0:T(1024)(128)(4,1)} %bitcast.54), calls=%async_computation.5 | async-start | bytes 8388608
  191.8 9.9 %slice-start.1 = ((s8[6291456]{0:T(1024)(128)(4,1)}), s8[2097152]{0:T(1024)(128)(4,1)S(1)}, s32[]{:S(2)}) async-start(s8[6291456]{0:T(1024)(128)(4,1)} %bitcast.54), calls=%async_computation.6 | async-start | bytes 4194304
  313.5 10.7 %copy-start = (f32[32,8]{0,1:T(8,128)S(1)}, f32[32,8]{0,1:T(8,128)}, u32[]{:S(2)}) copy-start(f32[32,8]{0,1:T(8,128)} %param.8) | copy-start | bytes 3076
  313.5 63.2 %all-to-all-start.1 = ((bf16[64,8,4096]{2,1,0:T(8,128)(2,1)}), bf16[64,8,4096]{2,1,0:T(8,128)(2,1)}, u32[]{:S(2)}, u32[]{:S(2)}) async-start(bf16[64,8,4096]{2,1,0:T(8,128)(2,1)} %bitcast.51), calls=%async_computation.2 | async-start | bytes 8388608 | tf_op jit(solution)/shard_map/all_to_all | solution.py:41
Sparse Core Ops, SparseCore 0:
  77.7 103.0 all-gather.1
  210.7 102.7 reduce-scatter.1
where the time goes:
time: 392 us
  waiting for transfers between devices  258 us (66%)
  blocking collectives  65.3 us (17%)
  matrix products  32.8 us (8%)
  between operations  13.6 us (3%)
  starting transfers between devices  10.8 us (3%)
  local copies, waits for them, and re-layouts  9.01 us (2%)
    all_gather x1, waiting for transfers between devices, on_device(): paired = lax.all_gather(arrived, 'sec', axis=0, tiled=True)  103 us
    reduce_scatter x1, waiting for transfers between devices, on_device(): lax.psum_scatter(jnp.dot(hidden_part, w_down[0], preferred_element_type=j...  103 us
    all_to_all x1, blocking collectives, on_device(): lax.all_to_all(outgoing, 'dev', split_axis=0, concat_axis=0, tiled=True)  65.3 us
    all_to_all x1, waiting for transfers between devices, on_device(): lax.all_to_all(expert_out, 'dev', split_axis=0, concat_axis=0, tiled=True)  52.3 us
    dot_general x1, matrix products, on_device(): up_part = jnp.dot(paired, w_up[0], preferred_element_type=jnp.float32)  11 us
    all_to_all x1, starting transfers between devices, on_device(): lax.all_to_all(expert_out, 'dev', split_axis=0, concat_axis=0, tiled=True)  10.6 us
    dot_general x1, matrix products, on_device(): gate_part = jnp.dot(paired, w_gate[0], preferred_element_type=jnp.float32)  9.88 us
    dot_general x1, matrix products, on_device(): jnp.dot(hidden_part, w_down[0], preferred_element_type=jnp.float32)  8.83 us
  transfers between devices with their start and end apart: 3, of which 3 were waited for; matrix products, arithmetic and copies ran while one was open for 0% of the time, Pallas kernels for 0%

commit v1 on v0

v1 whole, which is shorter than its diff:
```python
import jax
import jax.numpy as jnp
from jax import lax
from jax.experimental import pallas as pl
from jax.experimental.pallas import tpu as pltpu
from jax.sharding import PartitionSpec as P

MESH = pl.DeviceIdType.MESH
BF = jnp.bfloat16
F32 = jnp.float32

ROWS = 32
WIDTH = 4096
HALF = WIDTH // 2
CAP = 8
SLOTS = 2 * CAP
TOK = 2 * ROWS
INFO = 128
SHARE = 64
PARTS = (
    (0, 640, (0, 1, 2)),
    (640, 640, (1, 2, 0)),
    (1280, 768, (2, 0, 1)),
)
STEPS = (1, 3, 2)


def where_am_i():
    dev = lax.axis_index("dev")
    sec = lax.axis_index("sec")
    core = dev % 2
    z = (dev // 2) % 4
    y = ((dev // 8) % 2) * 2 + sec
    x = dev // 16
    return (x, y, z), core


def expert_of(x, y, z, core):
    return ((x * 2 + y // 2) * 4 + z) * 2 + core


def device(pos, core):
    x, y, z = pos
    return {"sec": y % 2, "dev": expert_of(x, y, z, core)}


def moved(pos, axis, to):
    return tuple(to if i == axis else v for i, v in enumerate(pos))


def greet(pos, core):
    barrier = pltpu.get_barrier_semaphore()
    count = 1
    pl.semaphore_signal(barrier, inc=1, device_id=device(pos, 1 - core), device_id_type=MESH)
    for axis in range(3):
        for o in STEPS:
            for c in range(2):
                to = device(moved(pos, axis, (pos[axis] + o) % 4), (core + c) % 2)
                pl.semaphore_signal(barrier, inc=1, device_id=to, device_id_type=MESH)
                count += 1
    pl.semaphore_wait(barrier, count)


def remote(src, dst, send, recv, to):
    return pltpu.make_async_remote_copy(
        src_ref=src, dst_ref=dst, send_sem=send, recv_sem=recv, device_id=to, device_id_type=MESH
    )


def line_expert(pos, axis, d):
    place, core = d // 2, d % 2
    x, y, z = moved(pos, axis, place)
    return expert_of(x, y, z, core)


def at_abc(ref, axes, a, b, lanes):
    index = [None] * 3
    index[axes[0]], index[axes[1]], index[axes[2]] = a, b, slice(None)
    return ref.at[index[0], index[1], index[2], :, lanes]


def lanes_of(p, core):
    first, size, _ = PARTS[p]
    return pl.ds(pl.multiple_of(core * HALF + first, 128), size)


def dispatch_kernel(
    hidden, routes, scores, xexp, i0, i1, i2,
    normed, mine, g0, g1, g2, y0, y1, y2,
    xs, xr, s1, r1, s2, r2, s3, r3, loc,
):
    pos, core = where_am_i()
    gs, ys, infos = (g0, g1, g2), (y0, y1, y2), (i0, i1, i2)
    greet(pos, core)

    values = hidden[...].astype(F32)
    scale = lax.rsqrt(jnp.mean(values * values, -1, keepdims=True) + 1e-06)
    normed[...] = (values * scale).astype(BF)
    share = scores[...] / jnp.sum(scores[...], -1, keepdims=True)
    chosen = routes[...]
    lane = lax.broadcasted_iota(jnp.int32, (ROWS, INFO), 1)
    used = jnp.zeros((ROWS, INFO), F32)
    shares = jnp.zeros((ROWS, INFO), F32)
    for k in range(chosen.shape[1]):
        e = chosen[:, k : k + 1]
        used = used + jnp.where(lane == e, 1.0, 0.0)
        shares = shares + jnp.where(lane == e + SHARE, share[:, k : k + 1], 0.0)
    below = (
        lax.broadcasted_iota(jnp.int32, (ROWS, ROWS), 1)
        < lax.broadcasted_iota(jnp.int32, (ROWS, ROWS), 0)
    ).astype(BF)
    place = jnp.dot(below, used.astype(BF), preferred_element_type=F32)
    mine[...] = jnp.where(lane < SHARE, used * (place + 1.0), shares).astype(BF)

    rows = pl.ds(pl.multiple_of(core * ROWS, ROWS), ROWS)
    partner = device(pos, 1 - core)
    swaps = []
    for p, (first, size, (A, B, C)) in enumerate(PARTS):
        own = gs[p].at[pos[B], pos[C], rows]
        other = remote(
            normed.at[:, lanes_of(p, 1 - core)], own.at[:, :size], xs.at[p, 0], xr.at[p, 0], partner
        )
        extra = remote(mine, own.at[:, size:], xs.at[p, 1], xr.at[p, 1], partner)
        other.start()
        extra.start()
        swaps += [(other, extra)]
        own[:, :size] = normed[:, lanes_of(p, core)]
        own[:, size:] = mine[...]
    first_copies, second_copies, third_copies, kept = {}, {}, {}, {}
    for p, (first, size, (A, B, C)) in enumerate(PARTS):
        for copy in swaps[p]:
            copy.wait_recv()
        for o in STEPS:
            block = gs[p].at[pos[B], pos[C]]
            copy = remote(
                block, block, s1.at[p, o], r1.at[p, o],
                device(moved(pos, C, (pos[C] + o) % 4), core),
            )
            copy.start()
            first_copies[p, o] = copy
    for p, (first, size, (A, B, C)) in enumerate(PARTS):
        for o in STEPS:
            first_copies[p, o].wait_recv()
        for o in STEPS:
            block = gs[p].at[pos[B]]
            copy = remote(
                block, block, s2.at[p, o], r2.at[p, o],
                device(moved(pos, B, (pos[B] + o) % 4), core),
            )
            copy.start()
            second_copies[p, o] = copy

    column = lax.broadcasted_iota(jnp.int32, (8 * 64, INFO), 1)
    drow = lax.broadcasted_iota(jnp.int32, (8 * 64, 1), 0)
    slot = drow % SLOTS
    chip = (drow % 64) // SLOTS
    source = lax.broadcasted_iota(jnp.int32, (1, 4 * TOK), 1)
    fits = (chip == source // TOK) & (slot // CAP == (source // ROWS) % 2)
    for j, b in enumerate((0,) + STEPS):
        for p, (first, size, (A, B, C)) in enumerate(PARTS):
            if b:
                second_copies[p, b].wait_recv()
            bsrc = (pos[B] + 4 - b) % 4
            block = gs[p].at[bsrc]
            info = block[:, :, size:].reshape(4 * TOK, INFO)
            pick = (column == line_expert(pos, A, drow // 64)).astype(BF)
            places = lax.dot_general(pick, info, (((1,), (1,)), ((), ())), preferred_element_type=F32)
            hot = (fits & (places == (slot % CAP + 1).astype(F32))).astype(BF)
            out = jnp.dot(
                hot, block[:, :, :size].reshape(4 * TOK, size), preferred_element_type=F32
            ).astype(BF)
            ys[p][j] = out.reshape(8, 4, SLOTS, size)
            for o in (2, 1, 3, 0):
                a = (pos[A] + o) % 4
                for c in range(2):
                    block_out = ys[p].at[j, 2 * a + (core + c) % 2]
                    target = at_abc(xexp, (A, B, C), pos[A], bsrc, lanes_of(p, core))
                    if o == 0 and c == 0:
                        copy = pltpu.make_async_copy(block_out, target, loc.at[p, j])
                        kept[p, j] = copy
                    else:
                        copy = remote(
                            block_out, target, s3.at[p, j, 2 * o + c], r3.at[p, j, 2 * o + c],
                            device(moved(pos, A, a), (core + c) % 2),
                        )
                        third_copies[p, j, o, c] = copy
                    copy.start()
    for p, (first, size, (A, B, C)) in enumerate(PARTS):
        infos[p][...] = gs[p][:, :, :, size:]
    for copy in kept.values():
        copy.wait()
    for copy in third_copies.values():
        copy.wait()
    for copies in (first_copies, second_copies):
        for copy in copies.values():
            copy.wait_send()
    for pair in swaps:
        for copy in pair:
            copy.wait_send()


def combine_kernel(
    eout, i0, i1, i2, out,
    q0, q1, q2, z0, z1, z2, t0, t1, t2, u0, u1, u2, v0, v1, v2, w, fin,
    s1, r1, s2, r2, s3, r3, loc, xs, xr,
):
    pos, core = where_am_i()
    infos = (i0, i1, i2)
    qs, zs, ts, us, vs = (q0, q1, q2), (z0, z1, z2), (t0, t1, t2), (u0, u1, u2), (v0, v1, v2)
    greet(pos, core)
    first_copies, second_copies, third_copies, kept = {}, {}, {}, {}
    order = (2, 1, 3, 0)
    for b in order:
        for p, (first, size, (A, B, C)) in enumerate(PARTS):
            bto = (pos[B] + b) % 4
            for o in (2, 1, 3, 0):
                a = (pos[A] + o) % 4
                for c in range(2):
                    source = at_abc(eout, (A, B, C), a, bto, lanes_of(p, (core + c) % 2))
                    target = qs[p].at[bto, 2 * pos[A] + core]
                    if o == 0 and c == 0:
                        copy = pltpu.make_async_copy(source, target, loc.at[p, b])
                        kept[p, b] = copy
                    else:
                        copy = remote(
                            source, target, s1.at[p, b, 2 * o + c], r1.at[p, b, 2 * o + c],
                            device(moved(pos, A, a), (core + c) % 2),
                        )
                        first_copies[p, b, o, c] = copy
                    copy.start()

    entry = lax.broadcasted_iota(jnp.int32, (INFO, 8 * 64), 0)
    dcol = lax.broadcasted_iota(jnp.int32, (1, 8 * 64), 1)
    slot = dcol % SLOTS
    chip = (dcol % 64) // SLOTS
    token = lax.broadcasted_iota(jnp.int32, (4 * TOK, 1), 0)
    fits = (chip == token // TOK) & (slot // CAP == (token // ROWS) % 2)
    for b in order:
        for p, (first, size, (A, B, C)) in enumerate(PARTS):
            bto = (pos[B] + b) % 4
            kept[p, b].wait()
            for o in range(4):
                for c in range(2):
                    if o or c:
                        first_copies[p, b, o, c].wait_recv()
            info = infos[p][bto].reshape(4 * TOK, INFO)
            expert = line_expert(pos, A, dcol // 64)
            places = jnp.dot(info, (entry == expert).astype(BF), preferred_element_type=F32)
            shares = jnp.dot(info, (entry == expert + SHARE).astype(BF), preferred_element_type=F32)
            hot = jnp.where(fits & (places == (slot % CAP + 1).astype(F32)), shares, 0.0).astype(BF)
            block = jnp.dot(
                hot, qs[p][bto].reshape(8 * 64, size), preferred_element_type=F32
            ).astype(BF)
            zs[p][bto] = block.reshape(4, TOK, size)
            if b:
                copy = remote(
                    zs[p].at[bto], ts[p].at[b], s2.at[p, b], r2.at[p, b],
                    device(moved(pos, B, bto), core),
                )
                copy.start()
                second_copies[p, b] = copy
    for p, (first, size, (A, B, C)) in enumerate(PARTS):
        total = zs[p][pos[B]].astype(F32)
        for o in STEPS:
            second_copies[p, o].wait_recv()
            total = total + ts[p][o].astype(F32)
        us[p][...] = total.astype(BF)
        for o in STEPS:
            cto = (pos[C] + o) % 4
            copy = remote(
                us[p].at[cto], vs[p].at[o], s3.at[p, o], r3.at[p, o],
                device(moved(pos, C, cto), core),
            )
            copy.start()
            third_copies[p, o] = copy
    partner = device(pos, 1 - core)
    swaps = []
    for p, (first, size, (A, B, C)) in enumerate(PARTS):
        total = us[p][pos[C]].astype(F32)
        for o in STEPS:
            third_copies[p, o].wait_recv()
            total = total + vs[p][o].astype(F32)
        w[:, first : first + size] = total.astype(BF)
        copy = remote(
            w.at[pl.ds(pl.multiple_of((1 - core) * ROWS, ROWS), ROWS), first : first + size],
            fin.at[:, lanes_of(p, core)], xs.at[p], xr.at[p], partner,
        )
        copy.start()
        swaps.append(copy)
    fin[:, pl.ds(pl.multiple_of(core * HALF, 128), HALF)] = w[
        pl.ds(pl.multiple_of(core * ROWS, ROWS), ROWS), :
    ]
    for copy in swaps:
        copy.wait()
    out[...] = fin[...]
    for copies in (first_copies, second_copies, third_copies):
        for copy in copies.values():
            copy.wait_send()


def vmem(*shape):
    return pltpu.VMEM(shape, BF)


def dma(*shape):
    return pltpu.SemaphoreType.DMA(shape)


def on_device(hidden_in, routes, scores, w_gate, w_up, w_down):
    sizes = [size for _, size, _ in PARTS]
    whole = pl.BlockSpec(memory_space=pltpu.VMEM)
    anywhere = pl.BlockSpec(memory_space=pl.ANY)
    xexp, i0, i1, i2 = pl.pallas_call(
        dispatch_kernel,
        out_shape=[jax.ShapeDtypeStruct((4, 4, 4, SLOTS, WIDTH), BF)]
        + [jax.ShapeDtypeStruct((4, 4, TOK, INFO), BF)] * 3,
        in_specs=[whole] * 3,
        out_specs=[anywhere] + [whole] * 3,
        scratch_shapes=[vmem(ROWS, WIDTH), vmem(ROWS, INFO)]
        + [vmem(4, 4, TOK, size + INFO) for size in sizes]
        + [vmem(4, 8, 4, SLOTS, size) for size in sizes]
        + [dma(3, 2), dma(3, 2), dma(3, 4), dma(3, 4), dma(3, 4), dma(3, 4)]
        + [dma(3, 4, 8), dma(3, 4, 8), dma(3, 4)],
        compiler_params=pltpu.CompilerParams(
            collective_id=0, has_side_effects=True, vmem_limit_bytes=48 * 1024 * 1024
        ),
        name="dispatch",
    )(hidden_in, routes, scores)
    rows = xexp.reshape(64 * SLOTS, WIDTH)
    gate_part = jnp.dot(rows, w_gate[0], preferred_element_type=F32)
    up_part = jnp.dot(rows, w_up[0], preferred_element_type=F32)
    hidden_part = (jax.nn.silu(gate_part) * up_part).astype(BF)
    result = jnp.dot(hidden_part, w_down[0], preferred_element_type=F32).astype(BF)
    return pl.pallas_call(
        combine_kernel,
        out_shape=jax.ShapeDtypeStruct((ROWS, WIDTH), BF),
        in_specs=[anywhere] + [whole] * 3,
        out_specs=whole,
        scratch_shapes=[vmem(4, 8, 4, SLOTS, size) for size in sizes]
        + [vmem(4, 4, TOK, size) for size in sizes] * 2
        + [vmem(4, TOK, size) for size in sizes] * 2
        + [vmem(TOK, HALF), vmem(ROWS, WIDTH)]
        + [dma(3, 4, 8), dma(3, 4, 8), dma(3, 4), dma(3, 4), dma(3, 4), dma(3, 4), dma(3, 4)]
        + [dma(3), dma(3)],
        compiler_params=pltpu.CompilerParams(
            collective_id=1, has_side_effects=True, vmem_limit_bytes=48 * 1024 * 1024
        ),
        name="combine",
    )(result.reshape(4, 4, 4, SLOTS, WIDTH), i0, i1, i2)


def solution(mesh):
    placed = (
        P(("sec", "dev"), None),
        P(("sec", "dev"), None),
        P(("sec", "dev"), None),
        P("dev", None, "sec"),
        P("dev", None, "sec"),
        P("dev", "sec", None),
    )
    return jax.shard_map(
        on_device, mesh=mesh, in_specs=placed, out_specs=P(("sec", "dev"), None), check_vma=False
    )
```

time: 392 us -> 165 us (0.42)
  waiting for transfers between devices: 258 us -> 0 us
  Pallas kernels: 0 us -> 134 us
  blocking collectives: 65.3 us -> 0 us
  between operations: 13.6 us -> 0.11 us
  starting transfers between devices: 10.8 us -> 0 us
  local copies, waits for them, and re-layouts: 9.01 us -> 3.2 us
  matrix products: 32.8 us -> 27.1 us
    pallas_call x0 -> x2, Pallas kernels: none -> 134 us  [the longest x1 71.5 us: on_device(): pl.pallas_call(dispatch_kernel, out_shape=[jax.ShapeDtypeStruct((4, 4, 4,...]
    all_gather x1 -> x0, waiting for transfers between devices: 103 us -> none  [on_device(): paired = lax.all_gather(arrived, 'sec', axis=0, tiled=True)]
    reduce_scatter x1 -> x0, waiting for transfers between devices: 103 us -> none  [on_device(): lax.psum_scatter(jnp.dot(hidden_part, w_down[0], preferred_element_type=j...]
    all_to_all x1 -> x0, blocking collectives: 65.3 us -> none  [on_device(): lax.all_to_all(outgoing, 'dev', split_axis=0, concat_axis=0, tiled=True)]
    all_to_all x1 -> x0, waiting for transfers between devices: 52.3 us -> none  [on_device(): lax.all_to_all(expert_out, 'dev', split_axis=0, concat_axis=0, tiled=True)]
    all_to_all x1 -> x0, starting transfers between devices: 10.6 us -> none  [on_device(): lax.all_to_all(expert_out, 'dev', split_axis=0, concat_axis=0, tiled=True)]
    gather x1 -> x0, local copies, waits for them, and re-layouts: 6.61 us -> none  [on_device(): jnp.take(returned, target.reshape(-1), axis=0)]
    dot_general x5 -> x3, matrix products: 32.8 us -> 27.1 us  [the longest x1 11.2 us: on_device(): up_part = jnp.dot(rows, w_up[0], preferred_element_type=F32)]
  transfers between devices with their start and end apart: 3 -> 0, of which waited for: 3 -> 0; matrix products, arithmetic and copies ran while one was open for 0% -> 0% of each run, Pallas kernels for 0% -> 0%
where the time goes in v1:
time: 165 us
  Pallas kernels  134 us (81%)
  matrix products  27.1 us (16%)
  local copies, waits for them, and re-layouts  3.2 us (2%)
    pallas_call x1, Pallas kernels, on_device(): pl.pallas_call(dispatch_kernel, out_shape=[jax.ShapeDtypeStruct((4, 4, 4,...  71.5 us
    pallas_call x1, Pallas kernels, on_device(): pl.pallas_call(combine_kernel, out_shape=jax.ShapeDtypeStruct((ROWS, WIDT...  62.7 us
    dot_general x1, matrix products, on_device(): up_part = jnp.dot(rows, w_up[0], preferred_element_type=F32)  11.2 us
    dot_general x1, matrix products, on_device(): jnp.dot(hidden_part, w_down[0], preferred_element_type=F32).astype(BF)  8.84 us
    dot_general x1, matrix products, on_device(): gate_part = jnp.dot(rows, w_gate[0], preferred_element_type=F32)  6.99 us

profile of v1, /device:TPU:1, one launch (start us, length us, event | category | flops | bytes accessed | tf_op | source)
XLA Modules:
  0.0 164.5 jit_solution(16467591278246832550)
XLA Ops:
  0.0 0.8 copy.7.routes
  0.8 0.8 copy.8.scores
  1.5 0.0 copy-start
  1.5 0.9 copy-done
  2.5 71.5 %dispatch.1 = (bf16[4,4,4,16,4096]{4,3,2,1,0:T(8,128)(2,1)}, bf16[4,4,64,128]{3,2,1,0:T(8,128)(2,1)S(1)}, bf16[4,4,64,128]{3,2,1,0:T(8,128)(2,1)S(1)}, bf16[4,4,64,128]{3,2,1,0:T(8,128)(2,1)S(1)}) custom-call(bf16[32,4096]{1,0:T(8,128)(2,1)S(1)} %copy-done, s32[32,8]{1,0:T(8,128)S(1)} %copy.7.routes, f32[32,8]{1,0:T(8,128)S(1)} %copy.8.scores), custom_call_target="tpu_custom_call" | custom-call | tf_op jit(solution)/shard_map/dispatch/pallas_call | solution.py:313
  73.9 0.0 copy-start.1
  74.0 0.0 copy-start.2
  74.0 0.0 slice-start
  74.0 11.2 %fusion.1 = f32[1024,768]{1,0:T(8,128)S(1)} fusion(bf16[1024,4096]{1,0:T(8,128)(2,1)} %bitcast.17, bf16[1,4096,768]{2,1,0:T(8,128)(2,1)} %param.10), kind=kOutput, calls=%fused_computation.2 | convolution fusion | flops 6442450944 | bytes 17825792 | tf_op jit(solution)/shard_map/dot_general | solution.py:331
  85.2 0.0 copy-done.1
  85.2 0.0 copy-done.2
  85.2 0.0 slice-start.1
  85.2 7.0 %multiply_convert_fusion = bf16[1024,768]{1,0:T(8,128)(2,1)S(1)} fusion(f32[1024,768]{1,0:T(8,128)S(1)} %fusion.1, bf16[1024,4096]{1,0:T(8,128)(2,1)S(1)} %bitcast.18, bf16[1,4096,768]{2,1,0:T(8,128)(2,1)S(1)} %copy-done.2), kind=kOutput, calls=%fused_computation.6 | convolution fusion | flops 6447169536 | bytes 19398656 | tf_op jit(solution)/shard_map/dot_general | solution.py:330
  92.2 0.0 slice-done
  92.3 0.0 slice-done.1
  92.3 8.8 %convolution_convert_fusion = bf16[1024,4096]{1,0:T(8,128)(2,1)} fusion(bf16[1024,768]{1,0:T(8,128)(2,1)S(1)} %multiply_convert_fusion, bf16[1,768,4096]{2,1,0:T(8,128)(2,1)S(1)} %bitcast.20), kind=kOutput, calls=%fused_computation | convolution fusion | flops 6446645248 | bytes 16252928 | tf_op jit(solution)/shard_map/dot_general | solution.py:333
  101.1 62.7 %combine.1 = bf16[32,4096]{1,0:T(8,128)(2,1)S(1)} custom-call(bf16[4,4,4,16,4096]{4,3,2,1,0:T(8,128)(2,1)} %bitcast.16, bf16[4,4,64,128]{3,2,1,0:T(8,128)(2,1)S(1)} %get-tuple-element.10.i0, bf16[4,4,64,128]{3,2,1,0:T(8,128)(2,1)S(1)} %get-tuple-element.11.i1, bf16[4,4,64,128]{3,2,1,0:T(8,128)(2,1)S(1)} %get-tuple-element.12.i2), custom_call_target="tpu_custom_call" | custom-call | tf_op jit(solution)/shard_map/combine/pallas_call | solution.py:334
  163.8 0.7 copy.10
  (1 shorter events, 0.0 us)
Async XLA Ops:
  1.5 0.9 copy-start
  73.9 11.3 %copy-start.1 = (bf16[4,4,4,16,4096]{4,3,2,1,0:T(8,128)(2,1)S(1)}, bf16[4,4,4,16,4096]{4,3,2,1,0:T(8,128)(2,1)}, u32[]{:S(2)}) copy-start(bf16[4,4,4,16,4096]{4,3,2,1,0:T(8,128)(2,1)} %get-tuple-element.9) | copy-start | bytes 25165828
  74.0 11.3 %copy-start.2 = (bf16[1,4096,768]{2,1,0:T(8,128)(2,1)S(1)}, bf16[1,4096,768]{2,1,0:T(8,128)(2,1)}, u32[]{:S(2)}) copy-start(bf16[1,4096,768]{2,1,0:T(8,128)(2,1)} %param.9) | copy-start | bytes 18874372
  74.0 18.3 %slice-start = ((s8[6291456]{0:T(1024)(128)(4,1)}), s8[4194304]{0:T(1024)(128)(4,1)S(1)}, s32[]{:S(2)}) async-start(s8[6291456]{0:T(1024)(128)(4,1)} %bitcast.19), calls=%async_computation | async-start | bytes 8388608
  85.2 7.0 %slice-start.1 = ((s8[6291456]{0:T(1024)(128)(4,1)}), s8[2097152]{0:T(1024)(128)(4,1)S(1)}, s32[]{:S(2)}) async-start(s8[6291456]{0:T(1024)(128)(4,1)} %bitcast.19), calls=%async_computation.1 | async-start | bytes 4194304

commit v2 on v0

v2 whole, which is shorter than its diff:
```python
import jax
import jax.numpy as jnp
from jax import lax
from jax.experimental import pallas as pl
from jax.experimental.pallas import tpu as pltpu
from jax.sharding import PartitionSpec as P

MESH = pl.DeviceIdType.MESH
BF = jnp.bfloat16
F32 = jnp.float32

ROWS = 32
WIDTH = 4096
HALF = WIDTH // 2
HIDDEN = 768
CAP = 8
SLOTS = 2 * CAP
TOK = 2 * ROWS
INFO = 128
SHARE = 64
AXES = ((0, 1, 2), (1, 2, 0), (2, 0, 1))
PARTS = ((0, 640), (640, 640), (1280, 768))
BACK = ((0, 768), (768, 640), (1408, 640))
STEPS = (1, 3, 2)
ORDER = (2, 1, 3, 0)


def where_am_i():
    dev = lax.axis_index("dev")
    sec = lax.axis_index("sec")
    core = dev % 2
    z = (dev // 2) % 4
    y = ((dev // 8) % 2) * 2 + sec
    x = dev // 16
    return (x, y, z), core


def expert_of(x, y, z, core):
    return ((x * 2 + y // 2) * 4 + z) * 2 + core


def device(pos, core):
    x, y, z = pos
    return {"sec": y % 2, "dev": expert_of(x, y, z, core)}


def moved(pos, axis, to):
    return tuple(to if i == axis else v for i, v in enumerate(pos))


def greet(pos, core):
    barrier = pltpu.get_barrier_semaphore()
    count = 1
    pl.semaphore_signal(barrier, inc=1, device_id=device(pos, 1 - core), device_id_type=MESH)
    for axis in range(3):
        for o in STEPS:
            for c in range(2):
                to = device(moved(pos, axis, (pos[axis] + o) % 4), (core + c) % 2)
                pl.semaphore_signal(barrier, inc=1, device_id=to, device_id_type=MESH)
                count += 1
    pl.semaphore_wait(barrier, count)


def remote(src, dst, send, recv, to):
    return pltpu.make_async_remote_copy(
        src_ref=src, dst_ref=dst, send_sem=send, recv_sem=recv, device_id=to, device_id_type=MESH
    )


def take(ref, sem):
    pltpu.make_async_copy(ref, ref, sem).wait()


def line_expert(pos, axis, d):
    place, core = d // 2, d % 2
    x, y, z = moved(pos, axis, place)
    return expert_of(x, y, z, core)


def half_rows(ref, h, axes, a, b, low, lanes):
    A, B, C = axes
    high, bit = [None] * 3, [None] * 3
    for axis, v in ((A, a), (B, b)):
        high[axis], bit[axis] = v // 2, v % 2
    high[C], bit[C] = slice(None), low
    return ref.at[h, high[0], bit[0], high[1], bit[1], high[2], :, lanes]


def lanes_of(part, core):
    first, size = part
    return pl.ds(pl.multiple_of(core * HALF + first, 128), size)


def kernel(
    hidden, routes, scores, w_gate, w_up, w_down, out,
    hid, rt, sc, gate, up, down, normed, mine,
    g0, g1, g2, y0, y1, y2, xexp, act,
    q0, q1, q2, t0, t1, t2, u0, u1, u2, v0, v1, v2, w, fin,
    ld, xs, xr, s1, r1, s2, r2, s3, r3, loc, bs1, br1, bloc, bs2, br2, bs3, br3, fs, fr,
):
    pos, core = where_am_i()
    gs, ys, qs = (g0, g1, g2), (y0, y1, y2), (q0, q1, q2)
    ts, us, vs = (t0, t1, t2), (u0, u1, u2), (v0, v1, v2)
    loads = [
        pltpu.make_async_copy(src, dst, ld.at[i])
        for i, (src, dst) in enumerate(
            (
                (hidden, hid), (routes, rt), (scores, sc),
                (w_gate.at[0], gate), (w_up.at[0], up), (w_down.at[0], down),
            )
        )
    ]
    for copy in loads[:3]:
        copy.start()
    greet(pos, core)
    for copy in loads[:3]:
        copy.wait()
    for copy in loads[3:]:
        copy.start()

    values = hid[...].astype(F32)
    scale = lax.rsqrt(jnp.mean(values * values, -1, keepdims=True) + 1e-06)
    normed[...] = (values * scale).astype(BF)
    share = sc[...] / jnp.sum(sc[...], 0, keepdims=True)
    chosen = rt[...]
    entry = lax.broadcasted_iota(jnp.int32, (INFO, ROWS), 0)
    used = jnp.zeros((INFO, ROWS), F32)
    shares = jnp.zeros((INFO, ROWS), F32)
    for k in range(chosen.shape[0]):
        e = chosen[k : k + 1]
        used = used + jnp.where(entry == e, 1.0, 0.0)
        shares = shares + jnp.where(entry == e + SHARE, share[k : k + 1], 0.0)
    ahead = lax.broadcasted_iota(jnp.int32, (ROWS, ROWS), 0)
    behind = lax.broadcasted_iota(jnp.int32, (ROWS, ROWS), 1)
    place = jnp.dot(
        used.astype(BF), (ahead < behind).astype(F32).astype(BF), preferred_element_type=F32
    )
    table = jnp.where(entry < SHARE, used * (place + 1.0), shares).astype(BF)
    mine[...] = lax.dot_general(
        (ahead == behind).astype(F32).astype(BF), table, (((1,), (1,)), ((), ())),
        preferred_element_type=F32,
    ).astype(BF)

    rows = pl.ds(pl.multiple_of(core * ROWS, ROWS), ROWS)
    partner = device(pos, 1 - core)
    swaps, first_copies, second_copies = [], {}, {}
    for p, (A, B, C) in enumerate(AXES):
        size = PARTS[p][1]
        own = gs[p].at[pos[B], pos[C] % 2, pos[C] // 2, rows]
        other = remote(
            normed.at[:, lanes_of(PARTS[p], 1 - core)], own.at[:, :size],
            xs.at[p, 0], xr.at[p, 0], partner,
        )
        extra = remote(mine, own.at[:, size:], xs.at[p, 1], xr.at[p, 1], partner)
        other.start()
        extra.start()
        swaps += [(other, extra)]
        own[:, :size] = normed[:, lanes_of(PARTS[p], core)]
        own[:, size:] = mine[...]
    for p, (A, B, C) in enumerate(AXES):
        for copy in swaps[p]:
            copy.wait_recv()
        for o in STEPS:
            block = gs[p].at[pos[B], pos[C] % 2, pos[C] // 2]
            copy = remote(
                block, block, s1.at[p, o], r1.at[p, o],
                device(moved(pos, C, (pos[C] + o) % 4), core),
            )
            copy.start()
            first_copies[p, o] = copy
    for p, (A, B, C) in enumerate(AXES):
        for o in STEPS:
            first_copies[p, o].wait_recv()
        for h in range(2):
            for o in STEPS:
                block = gs[p].at[pos[B], (h + pos[A] + pos[B]) % 2]
                copy = remote(
                    block, block, s2.at[p, h, o], r2.at[p, h, o],
                    device(moved(pos, B, (pos[B] + o) % 4), core),
                )
                copy.start()
                second_copies[p, h, o] = copy

    column = lax.broadcasted_iota(jnp.int32, (8 * 32, INFO), 1)
    drow = lax.broadcasted_iota(jnp.int32, (8 * 32, 1), 0)
    slot = drow % SLOTS
    source = lax.broadcasted_iota(jnp.int32, (1, 2 * TOK), 1)
    fits = ((drow % 32) // SLOTS == source // TOK) & (slot // CAP == (source // ROWS) % 2)
    wanted = (slot % CAP + 1).astype(F32)
    kept = {}
    for h in range(2):
        for j, b in enumerate((0,) + STEPS):
            for p, (A, B, C) in enumerate(AXES):
                size = PARTS[p][1]
                if b:
                    second_copies[p, h, b].wait_recv()
                bsrc = (pos[B] + 4 - b) % 4
                low = (h + pos[A] + bsrc) % 2
                block = gs[p].at[bsrc, low]
                info = block[:, :, size:].reshape(2 * TOK, INFO)
                pick = (column == line_expert(pos, A, drow // 32)).astype(F32).astype(BF)
                places = lax.dot_general(
                    pick, info, (((1,), (1,)), ((), ())), preferred_element_type=F32
                )
                hot = jnp.where(fits & (places == wanted), 1.0, 0.0).astype(BF)
                picked = jnp.dot(
                    hot, block[:, :, :size].reshape(2 * TOK, size), preferred_element_type=F32
                ).astype(BF)
                ys[p][h, j] = picked.reshape(8, 2, SLOTS, size)
                for o in ORDER:
                    a = (pos[A] + o) % 4
                    for c in range(2):
                        sent = ys[p].at[h, j, 2 * a + (core + c) % 2]
                        target = half_rows(
                            xexp, h, (A, B, C), pos[A], bsrc, low, lanes_of(PARTS[p], core)
                        )
                        if o == 0 and c == 0:
                            copy = pltpu.make_async_copy(sent, target, loc.at[p, h, j])
                            kept[p, h, j] = copy
                        else:
                            copy = remote(
                                sent, target, s3.at[p, h, j], r3.at[p, h, j],
                                device(moved(pos, A, a), (core + c) % 2),
                            )
                        copy.start()
    for pair in swaps:
        for copy in pair:
            copy.wait_send()
    for copies in (first_copies, second_copies):
        for copy in copies.values():
            copy.wait_send()

    back_kept = {}
    for h in range(2):
        for j in range(4):
            for p in range(3):
                kept[p, h, j].wait()
                take(ys[p].at[h, j, 0:7], r3.at[p, h, j])
        if h == 0:
            for copy in loads[3:]:
                copy.wait()

        @pl.loop(0, HIDDEN // 256)
        def _(n):
            cols = pl.ds(pl.multiple_of(n * 256, 256), 256)
            taken = xexp[h].reshape(512, WIDTH)
            gate_part = jnp.dot(taken, gate[:, cols], preferred_element_type=F32)
            up_part = jnp.dot(taken, up[:, cols], preferred_element_type=F32)
            act[:, cols] = (gate_part / (1.0 + jnp.exp(-gate_part)) * up_part).astype(BF)

        for c in (1, 0):
            for p, (A, B, C) in enumerate(AXES):
                lanes = lanes_of(BACK[p], (core + c) % 2)
                result = jnp.dot(act[...], down[:, lanes], preferred_element_type=F32).astype(BF)
                xexp[h, :, :, :, :, :, :, lanes] = result.reshape(
                    2, 2, 2, 2, 2, SLOTS, BACK[p][1]
                )
                for b in ORDER:
                    bto = (pos[B] + b) % 4
                    for o in ORDER:
                        a = (pos[A] + o) % 4
                        sent = half_rows(xexp, h, (A, B, C), a, bto, (h + a + bto) % 2, lanes)
                        target = qs[p].at[h, bto, 2 * pos[A] + core]
                        if o == 0 and c == 0:
                            copy = pltpu.make_async_copy(sent, target, bloc.at[p, h, b])
                            back_kept[p, h, b] = copy
                        else:
                            copy = remote(
                                sent, target, bs1.at[p, h, b], br1.at[p, h, b],
                                device(moved(pos, A, a), (core + c) % 2),
                            )
                        copy.start()

    entry = lax.broadcasted_iota(jnp.int32, (INFO, 8 * 32), 0)
    dcol = lax.broadcasted_iota(jnp.int32, (1, 8 * 32), 1)
    slot = dcol % SLOTS
    token = lax.broadcasted_iota(jnp.int32, (2 * TOK, 1), 0)
    fits = ((dcol % 32) // SLOTS == token // TOK) & (slot // CAP == (token // ROWS) % 2)
    wanted = (slot % CAP + 1).astype(F32)
    second_back, third_back = {}, {}
    for h in range(2):
        for b in ORDER:
            for p, (A, B, C) in enumerate(AXES):
                size, back = PARTS[p][1], BACK[p][1]
                bto = (pos[B] + b) % 4
                low = (h + pos[A] + bto) % 2
                back_kept[p, h, b].wait()
                take(qs[p].at[h, bto, 0:7], br1.at[p, h, b])
                info = gs[p].at[bto, low][:, :, size:].reshape(2 * TOK, INFO)
                expert = line_expert(pos, A, dcol // 32)
                places = jnp.dot(
                    info, (entry == expert).astype(F32).astype(BF), preferred_element_type=F32
                )
                weights = jnp.dot(
                    info, (entry == expert + SHARE).astype(F32).astype(BF),
                    preferred_element_type=F32,
                )
                hot = jnp.where(fits & (places == wanted), weights, 0.0).astype(BF)
                block = jnp.dot(
                    hot, qs[p][h, bto].reshape(8 * 32, back), preferred_element_type=F32
                ).astype(BF)
                if b:
                    ts[p][0, h, b] = block.reshape(2, TOK, back)
                    copy = remote(
                        ts[p].at[0, h, b], ts[p].at[1, h, b], bs2.at[p, h, b], br2.at[p, h, b],
                        device(moved(pos, B, bto), core),
                    )
                    copy.start()
                    second_back[p, h, b] = copy
                else:
                    ts[p][0, h, 0] = block.reshape(2, TOK, back)
    for h in range(2):
        for p, (A, B, C) in enumerate(AXES):
            total = ts[p][0, h, 0].astype(F32)
            for o in STEPS:
                second_back[p, h, o].wait_recv()
                total = total + ts[p][1, h, o].astype(F32)
            us[p][(h + pos[A] + pos[B]) % 2] = total.astype(BF)
    for p, (A, B, C) in enumerate(AXES):
        for o in STEPS:
            cto = (pos[C] + o) % 4
            copy = remote(
                us[p].at[cto % 2, cto // 2], vs[p].at[o], bs3.at[p, o], br3.at[p, o],
                device(moved(pos, C, cto), core),
            )
            copy.start()
            third_back[p, o] = copy
    finals = []
    for p, (A, B, C) in enumerate(AXES):
        first, back = BACK[p]
        total = us[p][pos[C] % 2, pos[C] // 2].astype(F32)
        for o in STEPS:
            third_back[p, o].wait_recv()
            total = total + vs[p][o].astype(F32)
        w[:, first : first + back] = total.astype(BF)
        copy = remote(
            w.at[pl.ds(pl.multiple_of((1 - core) * ROWS, ROWS), ROWS), first : first + back],
            fin.at[:, lanes_of(BACK[p], core)], fs.at[p], fr.at[p], partner,
        )
        copy.start()
        finals.append(copy)
    fin[:, pl.ds(pl.multiple_of(core * HALF, 128), HALF)] = w[rows, :]
    for copy in finals:
        copy.wait()
    out[...] = fin[...]
    for h in range(2):
        for p in range(3):
            for j in range(4):
                take(ys[p].at[h, j, 0:7], s3.at[p, h, j])
                take(qs[p].at[h, j, 0:7], bs1.at[p, h, j])
    for copies in (second_back, third_back):
        for copy in copies.values():
            copy.wait_send()


def vmem(*shape):
    return pltpu.VMEM(shape, BF)


def dma(*shape):
    return pltpu.SemaphoreType.DMA(shape)


def on_device(hidden_in, routes, scores, w_gate, w_up, w_down):
    sizes = [size for _, size in PARTS]
    backs = [size for _, size in BACK]
    top = routes.shape[1]
    anywhere = pl.BlockSpec(memory_space=pl.ANY)
    return pl.pallas_call(
        kernel,
        out_shape=jax.ShapeDtypeStruct((ROWS, WIDTH), BF),
        in_specs=[anywhere] * 6,
        out_specs=pl.BlockSpec(memory_space=pltpu.VMEM),
        scratch_shapes=[vmem(ROWS, WIDTH)]
        + [pltpu.VMEM((top, ROWS), jnp.int32), pltpu.VMEM((top, ROWS), F32)]
        + [vmem(WIDTH, HIDDEN), vmem(WIDTH, HIDDEN), vmem(HIDDEN, WIDTH)]
        + [vmem(ROWS, WIDTH), vmem(ROWS, INFO)]
        + [vmem(4, 2, 2, TOK, size + INFO) for size in sizes]
        + [vmem(2, 4, 8, 2, SLOTS, size) for size in sizes]
        + [vmem(2, 2, 2, 2, 2, 2, SLOTS, WIDTH), vmem(512, HIDDEN)]
        + [vmem(2, 4, 8, 2, SLOTS, size) for size in backs]
        + [vmem(2, 2, 4, 2, TOK, size) for size in backs]
        + [vmem(2, 2, TOK, size) for size in backs]
        + [vmem(4, TOK, size) for size in backs]
        + [vmem(TOK, HALF), vmem(ROWS, WIDTH)]
        + [dma(6), dma(3, 2), dma(3, 2), dma(3, 4), dma(3, 4), dma(3, 2, 4), dma(3, 2, 4)]
        + [dma(3, 2, 4)] * 6
        + [dma(3, 2, 4), dma(3, 2, 4), dma(3, 4), dma(3, 4), dma(3), dma(3)],
        compiler_params=pltpu.CompilerParams(
            collective_id=0, has_side_effects=True, vmem_limit_bytes=67_000_000
        ),
        name="experts",
    )(hidden_in, routes.T, scores.T, w_gate, w_up, w_down)


def solution(mesh):
    placed = (
        P(("sec", "dev"), None),
        P(("sec", "dev"), None),
        P(("sec", "dev"), None),
        P("dev", None, "sec"),
        P("dev", None, "sec"),
        P("dev", "sec", None),
    )
    return jax.shard_map(
        on_device, mesh=mesh, in_specs=placed, out_specs=P(("sec", "dev"), None), check_vma=False
    )
```

time: 392 us -> 128 us (0.33)
  waiting for transfers between devices: 258 us -> 0 us
  Pallas kernels: 0 us -> 126 us
  blocking collectives: 65.3 us -> 0 us
  matrix products: 32.8 us -> 0 us
  between operations: 13.6 us -> 0.01 us
  starting transfers between devices: 10.8 us -> 0 us
  local copies, waits for them, and re-layouts: 9.01 us -> 1.67 us
    pallas_call x0 -> x1, Pallas kernels: none -> 126 us  [on_device(): pl.pallas_call(kernel, out_shape=jax.ShapeDtypeStruct((ROWS, WIDTH), BF),...]
    all_gather x1 -> x0, waiting for transfers between devices: 103 us -> none  [on_device(): paired = lax.all_gather(arrived, 'sec', axis=0, tiled=True)]
    reduce_scatter x1 -> x0, waiting for transfers between devices: 103 us -> none  [on_device(): lax.psum_scatter(jnp.dot(hidden_part, w_down[0], preferred_element_type=j...]
    all_to_all x1 -> x0, blocking collectives: 65.3 us -> none  [on_device(): lax.all_to_all(outgoing, 'dev', split_axis=0, concat_axis=0, tiled=True)]
    all_to_all x1 -> x0, waiting for transfers between devices: 52.3 us -> none  [on_device(): lax.all_to_all(expert_out, 'dev', split_axis=0, concat_axis=0, tiled=True)]
    dot_general x5 -> x0, matrix products: 32.8 us -> none  [the longest x1 11 us: on_device(): up_part = jnp.dot(paired, w_up[0], preferred_element_type=jnp.float32)]
    all_to_all x1 -> x0, starting transfers between devices: 10.6 us -> none  [on_device(): lax.all_to_all(expert_out, 'dev', split_axis=0, concat_axis=0, tiled=True)]
    gather x1 -> x0, local copies, waits for them, and re-layouts: 6.61 us -> none  [on_device(): jnp.take(returned, target.reshape(-1), axis=0)]
  transfers between devices with their start and end apart: 3 -> 0, of which waited for: 3 -> 0; matrix products, arithmetic and copies ran while one was open for 0% -> 0% of each run, Pallas kernels for 0% -> 0%
where the time goes in v2:
time: 128 us
  Pallas kernels  126 us (98%)
  local copies, waits for them, and re-layouts  1.67 us (1%)
    pallas_call x1, Pallas kernels, on_device(): pl.pallas_call(kernel, out_shape=jax.ShapeDtypeStruct((ROWS, WIDTH), BF),...  126 us

profile of v2, /device:TPU:1, one launch (start us, length us, event | category | flops | bytes accessed | tf_op | source)
XLA Modules:
  0.0 127.6 jit_solution(7106029111041975532)
XLA Ops:
  0.0 125.9 %experts.1 = bf16[32,4096]{1,0:T(8,128)(2,1)} custom-call(bf16[32,4096]{1,0:T(8,128)(2,1)} %hidden.1, s32[8,32]{1,0:T(8,128)} %bitcast.2, f32[8,32]{1,0:T(8,128)} %bitcast.3, bf16[1,4096,768]{2,1,0:T(8,128)(2,1)} %w_gate.1, bf16[1,4096,768]{2,1,0:T(8,128)(2,1)} %w_up.1, bf16[1,768,4096]{2,1,0:T(8,128)(2,1)} %w_down.1), custom_call_target="tpu_custom_call" | custom-call | tf_op jit(solution)/shard_map/experts/pallas_call | solution.py:369
  125.9 1.7 %copy.8 = bf16[32,4096]{1,0:T(8,128)(2,1)} copy(bf16[32,4096]{1,0:T(8,128)(2,1)} %experts.1) | data formatting | bytes 524288

commit v3 on v2

--- a/solution.py
+++ b/solution.py
@@ -58,7 +58,7 @@
                 to = device(moved(pos, axis, (pos[axis] + o) % 4), (core + c) % 2)
                 pl.semaphore_signal(barrier, inc=1, device_id=to, device_id_type=MESH)
                 count += 1
-    pl.semaphore_wait(barrier, count)
+    return count
 
 
 def remote(src, dst, send, recv, to):
@@ -93,13 +93,13 @@
 
 def kernel(
     hidden, routes, scores, w_gate, w_up, w_down, out,
-    hid, rt, sc, gate, up, down, normed, mine,
+    hid, rt, sc, gate, up, down, m0, m1, m2,
     g0, g1, g2, y0, y1, y2, xexp, act,
-    q0, q1, q2, t0, t1, t2, u0, u1, u2, v0, v1, v2, w, fin,
-    ld, xs, xr, s1, r1, s2, r2, s3, r3, loc, bs1, br1, bloc, bs2, br2, bs3, br3, fs, fr,
+    q0, q1, q2, t0, t1, t2, u0, u1, u2, v0, v1, v2,
+    ld, s1, r1, s2, r2, f2, e2, s3, r3, loc, bs1, br1, bloc, bs2, br2, bs3, br3,
 ):
     pos, core = where_am_i()
-    gs, ys, qs = (g0, g1, g2), (y0, y1, y2), (q0, q1, q2)
+    ms, gs, ys, qs = (m0, m1, m2), (g0, g1, g2), (y0, y1, y2), (q0, q1, q2)
     ts, us, vs = (t0, t1, t2), (u0, u1, u2), (v0, v1, v2)
     loads = [
         pltpu.make_async_copy(src, dst, ld.at[i])
@@ -112,15 +112,12 @@
     ]
     for copy in loads[:3]:
         copy.start()
-    greet(pos, core)
+    peers = greet(pos, core)
     for copy in loads[:3]:
         copy.wait()
     for copy in loads[3:]:
         copy.start()
 
-    values = hid[...].astype(F32)
-    scale = lax.rsqrt(jnp.mean(values * values, -1, keepdims=True) + 1e-06)
-    normed[...] = (values * scale).astype(BF)
     share = sc[...] / jnp.sum(sc[...], 0, keepdims=True)
     chosen = rt[...]
     entry = lax.broadcasted_iota(jnp.int32, (INFO, ROWS), 0)
@@ -136,43 +133,40 @@
         used.astype(BF), (ahead < behind).astype(F32).astype(BF), preferred_element_type=F32
     )
     table = jnp.where(entry < SHARE, used * (place + 1.0), shares).astype(BF)
-    mine[...] = lax.dot_general(
+    mine = lax.dot_general(
         (ahead == behind).astype(F32).astype(BF), table, (((1,), (1,)), ((), ())),
         preferred_element_type=F32,
     ).astype(BF)
+    values = hid[...].astype(F32)
+    scale = lax.rsqrt(jnp.mean(values * values, -1, keepdims=True) + 1e-06)
+    normed = (values * scale).astype(BF)
+    for p, (first, size) in enumerate(PARTS):
+        for c in range(2):
+            ms[p][c, :, :size] = normed[:, c * HALF + first : c * HALF + first + size]
+            ms[p][c, :, size:] = mine
+    pl.semaphore_wait(pltpu.get_barrier_semaphore(), peers)
 
     rows = pl.ds(pl.multiple_of(core * ROWS, ROWS), ROWS)
-    partner = device(pos, 1 - core)
-    swaps, first_copies, second_copies = [], {}, {}
+    first_copies, second_copies, forwards = {}, {}, {}
     for p, (A, B, C) in enumerate(AXES):
-        size = PARTS[p][1]
         own = gs[p].at[pos[B], pos[C] % 2, pos[C] // 2, rows]
-        other = remote(
-            normed.at[:, lanes_of(PARTS[p], 1 - core)], own.at[:, :size],
-            xs.at[p, 0], xr.at[p, 0], partner,
-        )
-        extra = remote(mine, own.at[:, size:], xs.at[p, 1], xr.at[p, 1], partner)
-        other.start()
-        extra.start()
-        swaps += [(other, extra)]
-        own[:, :size] = normed[:, lanes_of(PARTS[p], core)]
-        own[:, size:] = mine[...]
+        for o in (2, 1, 3, 0):
+            for c in range(2):
+                if o or c:
+                    copy = remote(
+                        ms[p].at[(core + c) % 2], own, s1.at[p, o, c], r1.at[p, o, c],
+                        device(moved(pos, C, (pos[C] + o) % 4), (core + c) % 2),
+                    )
+                    copy.start()
+                    first_copies[p, o, c] = copy
+        own[...] = ms[p][core]
     for p, (A, B, C) in enumerate(AXES):
-        for copy in swaps[p]:
-            copy.wait_recv()
-        for o in STEPS:
-            block = gs[p].at[pos[B], pos[C] % 2, pos[C] // 2]
-            copy = remote(
-                block, block, s1.at[p, o], r1.at[p, o],
-                device(moved(pos, C, (pos[C] + o) % 4), core),
-            )
-            copy.start()
-            first_copies[p, o] = copy
-    for p, (A, B, C) in enumerate(AXES):
-        for o in STEPS:
-            first_copies[p, o].wait_recv()
+        for o in range(4):
+            for c in range(2):
+                if o or c:
+                    first_copies[p, o, c].wait_recv()
         for h in range(2):
-            for o in STEPS:
+            for o in (1, 3):
                 block = gs[p].at[pos[B], (h + pos[A] + pos[B]) % 2]
                 copy = remote(
                     block, block, s2.at[p, h, o], r2.at[p, h, o],
@@ -180,6 +174,19 @@
                 )
                 copy.start()
                 second_copies[p, h, o] = copy
+
+    def forward(h):
+        for p, (A, B, C) in enumerate(AXES):
+            for o in (1, 3):
+                second_copies[p, h, o].wait_recv()
+                bsrc = (pos[B] + 4 - o) % 4
+                piece = gs[p].at[bsrc, (h + pos[A] + bsrc) % 2, o // 2]
+                copy = remote(
+                    piece, piece, f2.at[p, h, o], e2.at[p, h, o],
+                    device(moved(pos, B, (pos[B] + o) % 4), core),
+                )
+                copy.start()
+                forwards[p, h, o] = copy
 
     column = lax.broadcasted_iota(jnp.int32, (8 * 32, INFO), 1)
     drow = lax.broadcasted_iota(jnp.int32, (8 * 32, 1), 0)
@@ -190,10 +197,13 @@
     kept = {}
     for h in range(2):
         for j, b in enumerate((0,) + STEPS):
+            if j == 1:
+                forward(h)
             for p, (A, B, C) in enumerate(AXES):
                 size = PARTS[p][1]
-                if b:
-                    second_copies[p, h, b].wait_recv()
+                if b == 2:
+                    for o in (1, 3):
+                        forwards[p, h, o].wait_recv()
                 bsrc = (pos[B] + 4 - b) % 4
                 low = (h + pos[A] + bsrc) % 2
                 block = gs[p].at[bsrc, low]
@@ -223,10 +233,7 @@
                                 device(moved(pos, A, a), (core + c) % 2),
                             )
                         copy.start()
-    for pair in swaps:
-        for copy in pair:
-            copy.wait_send()
-    for copies in (first_copies, second_copies):
+    for copies in (first_copies, second_copies, forwards):
         for copy in copies.values():
             copy.wait_send()
 
@@ -248,17 +255,19 @@
             up_part = jnp.dot(taken, up[:, cols], preferred_element_type=F32)
             act[:, cols] = (gate_part / (1.0 + jnp.exp(-gate_part)) * up_part).astype(BF)
 
-        for c in (1, 0):
-            for p, (A, B, C) in enumerate(AXES):
+        for p, (A, B, C) in enumerate(AXES):
+            for c in (1, 0):
                 lanes = lanes_of(BACK[p], (core + c) % 2)
                 result = jnp.dot(act[...], down[:, lanes], preferred_element_type=F32).astype(BF)
                 xexp[h, :, :, :, :, :, :, lanes] = result.reshape(
                     2, 2, 2, 2, 2, SLOTS, BACK[p][1]
                 )
-                for b in ORDER:
-                    bto = (pos[B] + b) % 4
-                    for o in ORDER:
-                        a = (pos[A] + o) % 4
+            for b in ORDER:
+                bto = (pos[B] + b) % 4
+                for o in ORDER:
+                    a = (pos[A] + o) % 4
+                    for c in (1, 0):
+                        lanes = lanes_of(BACK[p], (core + c) % 2)
                         sent = half_rows(xexp, h, (A, B, C), a, bto, (h + a + bto) % 2, lanes)
                         target = qs[p].at[h, bto, 2 * pos[A] + core]
                         if o == 0 and c == 0:
@@ -317,32 +326,27 @@
                 total = total + ts[p][1, h, o].astype(F32)
             us[p][(h + pos[A] + pos[B]) % 2] = total.astype(BF)
     for p, (A, B, C) in enumerate(AXES):
-        for o in STEPS:
+        for o in ORDER:
             cto = (pos[C] + o) % 4
-            copy = remote(
-                us[p].at[cto % 2, cto // 2], vs[p].at[o], bs3.at[p, o], br3.at[p, o],
-                device(moved(pos, C, cto), core),
-            )
-            copy.start()
-            third_back[p, o] = copy
-    finals = []
+            for c in range(2):
+                if o or c:
+                    to = (core + c) % 2
+                    copy = remote(
+                        us[p].at[cto % 2, cto // 2, pl.ds(pl.multiple_of(to * ROWS, ROWS), ROWS)],
+                        vs[p].at[o, c], bs3.at[p, o, c], br3.at[p, o, c],
+                        device(moved(pos, C, cto), to),
+                    )
+                    copy.start()
+                    third_back[p, o, c] = copy
     for p, (A, B, C) in enumerate(AXES):
-        first, back = BACK[p]
-        total = us[p][pos[C] % 2, pos[C] // 2].astype(F32)
-        for o in STEPS:
-            third_back[p, o].wait_recv()
-            total = total + vs[p][o].astype(F32)
-        w[:, first : first + back] = total.astype(BF)
-        copy = remote(
-            w.at[pl.ds(pl.multiple_of((1 - core) * ROWS, ROWS), ROWS), first : first + back],
-            fin.at[:, lanes_of(BACK[p], core)], fs.at[p], fr.at[p], partner,
-        )
-        copy.start()
-        finals.append(copy)
-    fin[:, pl.ds(pl.multiple_of(core * HALF, 128), HALF)] = w[rows, :]
-    for copy in finals:
-        copy.wait()
-    out[...] = fin[...]
+        vs[p][0, 0] = us[p][pos[C] % 2, pos[C] // 2, rows]
+        for c in range(2):
+            total = jnp.zeros((ROWS, BACK[p][1]), F32)
+            for o in range(4):
+                if o or c:
+                    third_back[p, o, c].wait_recv()
+                total = total + vs[p][o, c].astype(F32)
+            out[:, lanes_of(BACK[p], (core + c) % 2)] = total.astype(BF)
     for h in range(2):
         for p in range(3):
             for j in range(4):
@@ -374,18 +378,17 @@
         scratch_shapes=[vmem(ROWS, WIDTH)]
         + [pltpu.VMEM((top, ROWS), jnp.int32), pltpu.VMEM((top, ROWS), F32)]
         + [vmem(WIDTH, HIDDEN), vmem(WIDTH, HIDDEN), vmem(HIDDEN, WIDTH)]
-        + [vmem(ROWS, WIDTH), vmem(ROWS, INFO)]
+        + [vmem(2, ROWS, size + INFO) for size in sizes]
         + [vmem(4, 2, 2, TOK, size + INFO) for size in sizes]
         + [vmem(2, 4, 8, 2, SLOTS, size) for size in sizes]
         + [vmem(2, 2, 2, 2, 2, 2, SLOTS, WIDTH), vmem(512, HIDDEN)]
         + [vmem(2, 4, 8, 2, SLOTS, size) for size in backs]
         + [vmem(2, 2, 4, 2, TOK, size) for size in backs]
         + [vmem(2, 2, TOK, size) for size in backs]
-        + [vmem(4, TOK, size) for size in backs]
-        + [vmem(TOK, HALF), vmem(ROWS, WIDTH)]
-        + [dma(6), dma(3, 2), dma(3, 2), dma(3, 4), dma(3, 4), dma(3, 2, 4), dma(3, 2, 4)]
-        + [dma(3, 2, 4)] * 6
-        + [dma(3, 2, 4), dma(3, 2, 4), dma(3, 4), dma(3, 4), dma(3), dma(3)],
+        + [vmem(4, 2, ROWS, size) for size in backs]
+        + [dma(6), dma(3, 4, 2), dma(3, 4, 2)]
+        + [dma(3, 2, 4)] * 12
+        + [dma(3, 4, 2), dma(3, 4, 2)],
         compiler_params=pltpu.CompilerParams(
             collective_id=0, has_side_effects=True, vmem_limit_bytes=67_000_000
         ),

time: 128 us -> 122 us (0.953)
  Pallas kernels: 126 us -> 120 us
    pallas_call x1, Pallas kernels: 126 us -> 120 us  [on_device(): pl.pallas_call(kernel, out_shape=jax.ShapeDtypeStruct((ROWS, WIDTH), BF),...]
where the time goes in v3:
time: 122 us
  Pallas kernels  120 us (98%)
  local copies, waits for them, and re-layouts  1.67 us (1%)
    pallas_call x1, Pallas kernels, on_device(): pl.pallas_call(kernel, out_shape=jax.ShapeDtypeStruct((ROWS, WIDTH), BF),...  120 us

profile of v3, /device:TPU:1, one launch (start us, length us, event | category | flops | bytes accessed | tf_op | source)
XLA Modules:
  0.0 121.7 jit_solution(12604723598149280966)
XLA Ops:
  0.0 120.1 %experts.1 = bf16[32,4096]{1,0:T(8,128)(2,1)} custom-call(bf16[32,4096]{1,0:T(8,128)(2,1)} %hidden.1, s32[8,32]{1,0:T(8,128)} %bitcast.2, f32[8,32]{1,0:T(8,128)} %bitcast.3, bf16[1,4096,768]{2,1,0:T(8,128)(2,1)} %w_gate.1, bf16[1,4096,768]{2,1,0:T(8,128)(2,1)} %w_up.1, bf16[1,768,4096]{2,1,0:T(8,128)(2,1)} %w_down.1), custom_call_target="tpu_custom_call" | custom-call | tf_op jit(solution)/shard_map/experts/pallas_call | solution.py:373
  120.1 1.7 %copy.8 = bf16[32,4096]{1,0:T(8,128)(2,1)} copy(bf16[32,4096]{1,0:T(8,128)(2,1)} %experts.1) | data formatting | bytes 524288

commit v4 on v3

--- a/solution.py
+++ b/solution.py
@@ -286,7 +286,7 @@
     token = lax.broadcasted_iota(jnp.int32, (2 * TOK, 1), 0)
     fits = ((dcol % 32) // SLOTS == token // TOK) & (slot // CAP == (token // ROWS) % 2)
     wanted = (slot % CAP + 1).astype(F32)
-    second_back, third_back = {}, {}
+    second_back = {}
     for h in range(2):
         for b in ORDER:
             for p, (A, B, C) in enumerate(AXES):
@@ -324,37 +324,43 @@
             for o in STEPS:
                 second_back[p, h, o].wait_recv()
                 total = total + ts[p][1, h, o].astype(F32)
-            us[p][(h + pos[A] + pos[B]) % 2] = total.astype(BF)
-    for p, (A, B, C) in enumerate(AXES):
-        for o in ORDER:
-            cto = (pos[C] + o) % 4
-            for c in range(2):
-                if o or c:
+            low = (h + pos[A] + pos[B]) % 2
+            us[p][low] = total.astype(BF)
+            for high in range(2):
+                cto = 2 * high + low
+                o = (cto + 4 - pos[C]) % 4
+                for c in (1, 0):
                     to = (core + c) % 2
                     copy = remote(
-                        us[p].at[cto % 2, cto // 2, pl.ds(pl.multiple_of(to * ROWS, ROWS), ROWS)],
+                        us[p].at[low, high, pl.ds(pl.multiple_of(to * ROWS, ROWS), ROWS)],
                         vs[p].at[o, c], bs3.at[p, o, c], br3.at[p, o, c],
                         device(moved(pos, C, cto), to),
                     )
-                    copy.start()
-                    third_back[p, o, c] = copy
+                    if c:
+                        copy.start()
+                    else:
+                        pl.when(o != 0)(copy.start)
     for p, (A, B, C) in enumerate(AXES):
         vs[p][0, 0] = us[p][pos[C] % 2, pos[C] // 2, rows]
         for c in range(2):
             total = jnp.zeros((ROWS, BACK[p][1]), F32)
             for o in range(4):
                 if o or c:
-                    third_back[p, o, c].wait_recv()
+                    take(vs[p].at[o, c], br3.at[p, o, c])
                 total = total + vs[p][o, c].astype(F32)
             out[:, lanes_of(BACK[p], (core + c) % 2)] = total.astype(BF)
+    for p in range(3):
+        for o in range(4):
+            for c in range(2):
+                if o or c:
+                    take(vs[p].at[o, c], bs3.at[p, o, c])
     for h in range(2):
         for p in range(3):
             for j in range(4):
                 take(ys[p].at[h, j, 0:7], s3.at[p, h, j])
                 take(qs[p].at[h, j, 0:7], bs1.at[p, h, j])
-    for copies in (second_back, third_back):
-        for copy in copies.values():
-            copy.wait_send()
+    for copy in second_back.values():
+        copy.wait_send()
 
 
 def vmem(*shape):
@@ -372,7 +378,7 @@
     anywhere = pl.BlockSpec(memory_space=pl.ANY)
     return pl.pallas_call(
         kernel,
-        out_shape=jax.ShapeDtypeStruct((ROWS, WIDTH), BF),
+        out_shape=pltpu.VMEM((ROWS, WIDTH), BF),
         in_specs=[anywhere] * 6,
         out_specs=pl.BlockSpec(memory_space=pltpu.VMEM),
         scratch_shapes=[vmem(ROWS, WIDTH)]
@@ -390,7 +396,7 @@
         + [dma(3, 2, 4)] * 12
         + [dma(3, 4, 2), dma(3, 4, 2)],
         compiler_params=pltpu.CompilerParams(
-            collective_id=0, has_side_effects=True, vmem_limit_bytes=67_000_000
+            collective_id=0, has_side_effects=True, vmem_limit_bytes=62_500_000
         ),
         name="experts",
     )(hidden_in, routes.T, scores.T, w_gate, w_up, w_down)

time: 122 us -> 119 us (0.975)
  Pallas kernels: 120 us -> 117 us
    pallas_call x1, Pallas kernels: 120 us -> 117 us  [on_device(): pl.pallas_call(kernel, out_shape=pltpu.VMEM((ROWS, WIDTH), BF), in_specs=...]
where the time goes in v4:
time: 119 us; the launch traced here: 118 us
  Pallas kernels  117 us (98%)
    pallas_call x1, Pallas kernels, on_device(): pl.pallas_call(kernel, out_shape=pltpu.VMEM((ROWS, WIDTH), BF), in_specs=...  117 us

profile of v4, /device:TPU:1, one launch (start us, length us, event | category | flops | bytes accessed | tf_op | source)
XLA Modules:
  0.0 117.7 jit_solution(5751623775902660079)
XLA Ops:
  0.0 116.9 %experts.1 = bf16[32,4096]{1,0:T(8,128)(2,1)S(1)} custom-call(bf16[32,4096]{1,0:T(8,128)(2,1)} %hidden.1, s32[8,32]{1,0:T(8,128)} %bitcast.2, f32[8,32]{1,0:T(8,128)} %bitcast.3, bf16[1,4096,768]{2,1,0:T(8,128)(2,1)} %w_gate.1, bf16[1,4096,768]{2,1,0:T(8,128)(2,1)} %w_up.1, bf16[1,768,4096]{2,1,0:T(8,128)(2,1)} %w_down.1), custom_call_target="tpu_custom_call" | custom-call | tf_op jit(solution)/shard_map/experts/pallas_call | solution.py:379
  116.9 0.7 copy.8

commit v5 on v4

--- a/solution.py
+++ b/solution.py
@@ -96,7 +96,7 @@
     hid, rt, sc, gate, up, down, m0, m1, m2,
     g0, g1, g2, y0, y1, y2, xexp, act,
     q0, q1, q2, t0, t1, t2, u0, u1, u2, v0, v1, v2,
-    ld, s1, r1, s2, r2, f2, e2, s3, r3, loc, bs1, br1, bloc, bs2, br2, bs3, br3,
+    ld, s1, r1, es, s2, r2, f2, e2, s3, r3, loc, bs1, br1, bloc, bs2, br2, bs3, br3,
 ):
     pos, core = where_am_i()
     ms, gs, ys, qs = (m0, m1, m2), (g0, g1, g2), (y0, y1, y2), (q0, q1, q2)
@@ -147,7 +147,7 @@
     pl.semaphore_wait(pltpu.get_barrier_semaphore(), peers)
 
     rows = pl.ds(pl.multiple_of(core * ROWS, ROWS), ROWS)
-    first_copies, second_copies, forwards = {}, {}, {}
+    first_copies, early, second_copies, forwards = {}, {}, {}, {}
     for p, (A, B, C) in enumerate(AXES):
         own = gs[p].at[pos[B], pos[C] % 2, pos[C] // 2, rows]
         for o in (2, 1, 3, 0):
@@ -161,26 +161,40 @@
                     first_copies[p, o, c] = copy
         own[...] = ms[p][core]
     for p, (A, B, C) in enumerate(AXES):
+        own = gs[p].at[pos[B], pos[C] % 2, pos[C] // 2, rows]
+        h = (pos[A] + pos[B] + pos[C]) % 2
+        for o in (1, 3):
+            for c in range(2):
+                copy = remote(
+                    ms[p].at[(core + c) % 2], own, es.at[p, o, c], r2.at[p, h, o, pos[C] // 2],
+                    device(moved(pos, B, (pos[B] + o) % 4), (core + c) % 2),
+                )
+                copy.start()
+                early[p, o, c] = copy
+    for p, (A, B, C) in enumerate(AXES):
         for o in range(4):
             for c in range(2):
                 if o or c:
                     first_copies[p, o, c].wait_recv()
         for h in range(2):
+            low = (h + pos[A] + pos[B]) % 2
             for o in (1, 3):
-                block = gs[p].at[pos[B], (h + pos[A] + pos[B]) % 2]
-                copy = remote(
-                    block, block, s2.at[p, h, o], r2.at[p, h, o],
-                    device(moved(pos, B, (pos[B] + o) % 4), core),
-                )
-                copy.start()
-                second_copies[p, h, o] = copy
+                for high in range(2):
+                    block = gs[p].at[pos[B], low, high]
+                    copy = remote(
+                        block, block, s2.at[p, h, o, high], r2.at[p, h, o, high],
+                        device(moved(pos, B, (pos[B] + o) % 4), core),
+                    )
+                    rest = 2 * high + low != pos[C]
+                    pl.when(rest)(copy.start)
+                    second_copies[p, h, o, high] = rest, copy
 
     def forward(h):
         for p, (A, B, C) in enumerate(AXES):
             for o in (1, 3):
-                second_copies[p, h, o].wait_recv()
                 bsrc = (pos[B] + 4 - o) % 4
                 piece = gs[p].at[bsrc, (h + pos[A] + bsrc) % 2, o // 2]
+                take(piece, r2.at[p, h, o, o // 2])
                 copy = remote(
                     piece, piece, f2.at[p, h, o], e2.at[p, h, o],
                     device(moved(pos, B, (pos[B] + o) % 4), core),
@@ -207,6 +221,8 @@
                 bsrc = (pos[B] + 4 - b) % 4
                 low = (h + pos[A] + bsrc) % 2
                 block = gs[p].at[bsrc, low]
+                if b in (1, 3):
+                    take(block.at[1 - b // 2], r2.at[p, h, b, 1 - b // 2])
                 info = block[:, :, size:].reshape(2 * TOK, INFO)
                 pick = (column == line_expert(pos, A, drow // 32)).astype(F32).astype(BF)
                 places = lax.dot_general(
@@ -233,9 +249,11 @@
                                 device(moved(pos, A, a), (core + c) % 2),
                             )
                         copy.start()
-    for copies in (first_copies, second_copies, forwards):
+    for copies in (first_copies, early, forwards):
         for copy in copies.values():
             copy.wait_send()
+    for rest, copy in second_copies.values():
+        pl.when(rest)(copy.wait_send)
 
     back_kept = {}
     for h in range(2):
@@ -287,41 +305,53 @@
     fits = ((dcol % 32) // SLOTS == token // TOK) & (slot // CAP == (token // ROWS) % 2)
     wanted = (slot % CAP + 1).astype(F32)
     second_back = {}
-    for h in range(2):
-        for b in ORDER:
-            for p, (A, B, C) in enumerate(AXES):
-                size, back = PARTS[p][1], BACK[p][1]
-                bto = (pos[B] + b) % 4
-                low = (h + pos[A] + bto) % 2
-                back_kept[p, h, b].wait()
-                take(qs[p].at[h, bto, 0:7], br1.at[p, h, b])
-                info = gs[p].at[bto, low][:, :, size:].reshape(2 * TOK, INFO)
-                expert = line_expert(pos, A, dcol // 32)
-                places = jnp.dot(
-                    info, (entry == expert).astype(F32).astype(BF), preferred_element_type=F32
-                )
-                weights = jnp.dot(
-                    info, (entry == expert + SHARE).astype(F32).astype(BF),
-                    preferred_element_type=F32,
-                )
-                hot = jnp.where(fits & (places == wanted), weights, 0.0).astype(BF)
-                block = jnp.dot(
-                    hot, qs[p][h, bto].reshape(8 * 32, back), preferred_element_type=F32
-                ).astype(BF)
-                if b:
-                    ts[p][0, h, b] = block.reshape(2, TOK, back)
-                    copy = remote(
-                        ts[p].at[0, h, b], ts[p].at[1, h, b], bs2.at[p, h, b], br2.at[p, h, b],
-                        device(moved(pos, B, bto), core),
-                    )
-                    copy.start()
-                    second_back[p, h, b] = copy
-                else:
-                    ts[p][0, h, 0] = block.reshape(2, TOK, back)
-    for h in range(2):
+
+    def weigh(h, b, p):
+        A, B, C = AXES[p]
+        size, back = PARTS[p][1], BACK[p][1]
+        bto = (pos[B] + b) % 4
+        back_kept[p, h, b].wait()
+        take(qs[p].at[h, bto, 0:7], br1.at[p, h, b])
+        info = gs[p].at[bto, (h + pos[A] + bto) % 2][:, :, size:].reshape(2 * TOK, INFO)
+        expert = line_expert(pos, A, dcol // 32)
+        places = jnp.dot(
+            info, (entry == expert).astype(F32).astype(BF), preferred_element_type=F32
+        )
+        weights = jnp.dot(
+            info, (entry == expert + SHARE).astype(F32).astype(BF), preferred_element_type=F32
+        )
+        hot = jnp.where(fits & (places == wanted), weights, 0.0).astype(BF)
+        return jnp.dot(hot, qs[p][h, bto].reshape(8 * 32, back), preferred_element_type=F32)
+
+    def pass_on(h, b, p, src, dst, which):
+        to = device(moved(pos, AXES[p][1], (pos[AXES[p][1]] + b) % 4), core)
+        copy = remote(src, dst, bs2.at[p, h, which], br2.at[p, h, which], to)
+        copy.start()
+        second_back[p, h, which] = copy
+
+    for p in range(3):
+        ts[p][0, 0, 2] = weigh(0, 2, p).astype(BF).reshape(2, TOK, BACK[p][1])
+        pass_on(0, 1, p, ts[p].at[0, 0, 2, 0], ts[p].at[1, 0, 2, 0], 2)
+        pass_on(0, 3, p, ts[p].at[0, 0, 2, 1], ts[p].at[1, 0, 2, 1], 0)
+    for p in range(3):
+        ts[p][0, 0, 0] = weigh(0, 0, p).astype(BF).reshape(2, TOK, BACK[p][1])
+    for b in ORDER:
+        for p in range(3):
+            ts[p][0, 1, b] = weigh(1, b, p).astype(BF).reshape(2, TOK, BACK[p][1])
+            if b:
+                pass_on(1, b, p, ts[p].at[0, 1, b], ts[p].at[1, 1, b], b)
+    for b, which in ((1, 2), (3, 0)):
+        for p in range(3):
+            high = b // 2
+            block = weigh(0, b, p).reshape(2, TOK, BACK[p][1])
+            second_back[p, 0, which].wait_recv()
+            ts[p][0, 0, b, high] = (block[high] + ts[p][1, 0, 2, high].astype(F32)).astype(BF)
+            ts[p][0, 0, b, 1 - high] = block[1 - high].astype(BF)
+            pass_on(0, b, p, ts[p].at[0, 0, b], ts[p].at[1, 0, b], b)
+    for h in (1, 0):
         for p, (A, B, C) in enumerate(AXES):
             total = ts[p][0, h, 0].astype(F32)
-            for o in STEPS:
+            for o in STEPS if h else (1, 3):
                 second_back[p, h, o].wait_recv()
                 total = total + ts[p][1, h, o].astype(F32)
             low = (h + pos[A] + pos[B]) % 2
@@ -393,7 +423,8 @@
         + [vmem(2, 2, TOK, size) for size in backs]
         + [vmem(4, 2, ROWS, size) for size in backs]
         + [dma(6), dma(3, 4, 2), dma(3, 4, 2)]
-        + [dma(3, 2, 4)] * 12
+        + [dma(3, 4, 2), dma(3, 2, 4, 2), dma(3, 2, 4, 2)]
+        + [dma(3, 2, 4)] * 10
         + [dma(3, 4, 2), dma(3, 4, 2)],
         compiler_params=pltpu.CompilerParams(
             collective_id=0, has_side_effects=True, vmem_limit_bytes=62_500_000

time: 119 us -> 118 us (level)
  no operation moved by 1% of the time
where the time goes in v5:
time: 118 us
  Pallas kernels  117 us (99%)
    pallas_call x1, Pallas kernels, on_device(): pl.pallas_call(kernel, out_shape=pltpu.VMEM((ROWS, WIDTH), BF), in_specs=...  117 us

profile of v5, /device:TPU:1, one launch (start us, length us, event | category | flops | bytes accessed | tf_op | source)
XLA Modules:
  0.0 117.6 jit_solution(16897920631280455015)
XLA Ops:
  0.0 116.8 %experts.1 = bf16[32,4096]{1,0:T(8,128)(2,1)S(1)} custom-call(bf16[32,4096]{1,0:T(8,128)(2,1)} %hidden.1, s32[8,32]{1,0:T(8,128)} %bitcast.2, f32[8,32]{1,0:T(8,128)} %bitcast.3, bf16[1,4096,768]{2,1,0:T(8,128)(2,1)} %w_gate.1, bf16[1,4096,768]{2,1,0:T(8,128)(2,1)} %w_up.1, bf16[1,768,4096]{2,1,0:T(8,128)(2,1)} %w_down.1), custom_call_target="tpu_custom_call" | custom-call | tf_op jit(solution)/shard_map/experts/pallas_call | solution.py:409
  116.9 0.7 copy.8

commit v6 on v5

--- a/solution.py
+++ b/solution.py
@@ -113,10 +113,8 @@
     for copy in loads[:3]:
         copy.start()
     peers = greet(pos, core)
-    for copy in loads[:3]:
+    for copy in loads[1:3]:
         copy.wait()
-    for copy in loads[3:]:
-        copy.start()
 
     share = sc[...] / jnp.sum(sc[...], 0, keepdims=True)
     chosen = rt[...]
@@ -137,6 +135,7 @@
         (ahead == behind).astype(F32).astype(BF), table, (((1,), (1,)), ((), ())),
         preferred_element_type=F32,
     ).astype(BF)
+    loads[0].wait()
     values = hid[...].astype(F32)
     scale = lax.rsqrt(jnp.mean(values * values, -1, keepdims=True) + 1e-06)
     normed = (values * scale).astype(BF)
@@ -189,6 +188,9 @@
                     pl.when(rest)(copy.start)
                     second_copies[p, h, o, high] = rest, copy
 
+    for copy in loads[3:]:
+        copy.start()
+
     def forward(h):
         for p, (A, B, C) in enumerate(AXES):
             for o in (1, 3):
@@ -211,8 +213,8 @@
     kept = {}
     for h in range(2):
         for j, b in enumerate((0,) + STEPS):
-            if j == 1:
-                forward(h)
+            if h == 0 and j in (1, 2):
+                forward(j - 1)
             for p, (A, B, C) in enumerate(AXES):
                 size = PARTS[p][1]
                 if b == 2:

time: 118 us -> 115 us (0.975)
  Pallas kernels: 117 us -> 114 us
    pallas_call x1, Pallas kernels: 117 us -> 114 us  [on_device(): pl.pallas_call(kernel, out_shape=pltpu.VMEM((ROWS, WIDTH), BF), in_specs=...]
where the time goes in v6:
time: 115 us
  Pallas kernels  114 us (99%)
    pallas_call x1, Pallas kernels, on_device(): pl.pallas_call(kernel, out_shape=pltpu.VMEM((ROWS, WIDTH), BF), in_specs=...  114 us

profile of v6, /device:TPU:1, one launch (start us, length us, event | category | flops | bytes accessed | tf_op | source)
XLA Modules:
  0.0 115.2 jit_solution(13161587928657988302)
XLA Ops:
  0.0 114.4 %experts.1 = bf16[32,4096]{1,0:T(8,128)(2,1)S(1)} custom-call(bf16[32,4096]{1,0:T(8,128)(2,1)} %hidden.1, s32[8,32]{1,0:T(8,128)} %bitcast.2, f32[8,32]{1,0:T(8,128)} %bitcast.3, bf16[1,4096,768]{2,1,0:T(8,128)(2,1)} %w_gate.1, bf16[1,4096,768]{2,1,0:T(8,128)(2,1)} %w_up.1, bf16[1,768,4096]{2,1,0:T(8,128)(2,1)} %w_down.1), custom_call_target="tpu_custom_call" | custom-call | tf_op jit(solution)/shard_map/experts/pallas_call | solution.py:411
  114.4 0.7 copy.8

commit v7 on v6

--- a/solution.py
+++ b/solution.py
@@ -258,6 +258,37 @@
         pl.when(rest)(copy.wait_send)
 
     back_kept = {}
+    entry = lax.broadcasted_iota(jnp.int32, (INFO, 8 * 32), 0)
+    dcol = lax.broadcasted_iota(jnp.int32, (1, 8 * 32), 1)
+    slot = dcol % SLOTS
+    token = lax.broadcasted_iota(jnp.int32, (2 * TOK, 1), 0)
+    fits = ((dcol % 32) // SLOTS == token // TOK) & (slot // CAP == (token // ROWS) % 2)
+    wanted = (slot % CAP + 1).astype(F32)
+    second_back = {}
+
+    def weigh(h, b, p):
+        A, B, C = AXES[p]
+        size, back = PARTS[p][1], BACK[p][1]
+        bto = (pos[B] + b) % 4
+        back_kept[p, h, b].wait()
+        take(qs[p].at[h, bto, 0:7], br1.at[p, h, b])
+        info = gs[p].at[bto, (h + pos[A] + bto) % 2][:, :, size:].reshape(2 * TOK, INFO)
+        expert = line_expert(pos, A, dcol // 32)
+        places = jnp.dot(
+            info, (entry == expert).astype(F32).astype(BF), preferred_element_type=F32
+        )
+        weights = jnp.dot(
+            info, (entry == expert + SHARE).astype(F32).astype(BF), preferred_element_type=F32
+        )
+        hot = jnp.where(fits & (places == wanted), weights, 0.0).astype(BF)
+        return jnp.dot(hot, qs[p][h, bto].reshape(8 * 32, back), preferred_element_type=F32)
+
+    def pass_on(h, b, p, src, dst, which):
+        to = device(moved(pos, AXES[p][1], (pos[AXES[p][1]] + b) % 4), core)
+        copy = remote(src, dst, bs2.at[p, h, which], br2.at[p, h, which], to)
+        copy.start()
+        second_back[p, h, which] = copy
+
     for h in range(2):
         for j in range(4):
             for p in range(3):
@@ -275,6 +306,11 @@
             up_part = jnp.dot(taken, up[:, cols], preferred_element_type=F32)
             act[:, cols] = (gate_part / (1.0 + jnp.exp(-gate_part)) * up_part).astype(BF)
 
+        if h == 1:
+            for p in range(3):
+                ts[p][0, 0, 2] = weigh(0, 2, p).astype(BF).reshape(2, TOK, BACK[p][1])
+                pass_on(0, 1, p, ts[p].at[0, 0, 2, 0], ts[p].at[1, 0, 2, 0], 2)
+                pass_on(0, 3, p, ts[p].at[0, 0, 2, 1], ts[p].at[1, 0, 2, 1], 0)
         for p, (A, B, C) in enumerate(AXES):
             for c in (1, 0):
                 lanes = lanes_of(BACK[p], (core + c) % 2)
@@ -300,48 +336,8 @@
                             )
                         copy.start()
 
-    entry = lax.broadcasted_iota(jnp.int32, (INFO, 8 * 32), 0)
-    dcol = lax.broadcasted_iota(jnp.int32, (1, 8 * 32), 1)
-    slot = dcol % SLOTS
-    token = lax.broadcasted_iota(jnp.int32, (2 * TOK, 1), 0)
-    fits = ((dcol % 32) // SLOTS == token // TOK) & (slot // CAP == (token // ROWS) % 2)
-    wanted = (slot % CAP + 1).astype(F32)
-    second_back = {}
-
-    def weigh(h, b, p):
-        A, B, C = AXES[p]
-        size, back = PARTS[p][1], BACK[p][1]
-        bto = (pos[B] + b) % 4
-        back_kept[p, h, b].wait()
-        take(qs[p].at[h, bto, 0:7], br1.at[p, h, b])
-        info = gs[p].at[bto, (h + pos[A] + bto) % 2][:, :, size:].reshape(2 * TOK, INFO)
-        expert = line_expert(pos, A, dcol // 32)
-        places = jnp.dot(
-            info, (entry == expert).astype(F32).astype(BF), preferred_element_type=F32
-        )
-        weights = jnp.dot(
-            info, (entry == expert + SHARE).astype(F32).astype(BF), preferred_element_type=F32
-        )
-        hot = jnp.where(fits & (places == wanted), weights, 0.0).astype(BF)
-        return jnp.dot(hot, qs[p][h, bto].reshape(8 * 32, back), preferred_element_type=F32)
-
-    def pass_on(h, b, p, src, dst, which):
-        to = device(moved(pos, AXES[p][1], (pos[AXES[p][1]] + b) % 4), core)
-        copy = remote(src, dst, bs2.at[p, h, which], br2.at[p, h, which], to)
-        copy.start()
-        second_back[p, h, which] = copy
-
-    for p in range(3):
-        ts[p][0, 0, 2] = weigh(0, 2, p).astype(BF).reshape(2, TOK, BACK[p][1])
-        pass_on(0, 1, p, ts[p].at[0, 0, 2, 0], ts[p].at[1, 0, 2, 0], 2)
-        pass_on(0, 3, p, ts[p].at[0, 0, 2, 1], ts[p].at[1, 0, 2, 1], 0)
     for p in range(3):
         ts[p][0, 0, 0] = weigh(0, 0, p).astype(BF).reshape(2, TOK, BACK[p][1])
-    for b in ORDER:
-        for p in range(3):
-            ts[p][0, 1, b] = weigh(1, b, p).astype(BF).reshape(2, TOK, BACK[p][1])
-            if b:
-                pass_on(1, b, p, ts[p].at[0, 1, b], ts[p].at[1, 1, b], b)
     for b, which in ((1, 2), (3, 0)):
         for p in range(3):
             high = b // 2
@@ -350,7 +346,12 @@
             ts[p][0, 0, b, high] = (block[high] + ts[p][1, 0, 2, high].astype(F32)).astype(BF)
             ts[p][0, 0, b, 1 - high] = block[1 - high].astype(BF)
             pass_on(0, b, p, ts[p].at[0, 0, b], ts[p].at[1, 0, b], b)
-    for h in (1, 0):
+    for b in ORDER:
+        for p in range(3):
+            ts[p][0, 1, b] = weigh(1, b, p).astype(BF).reshape(2, TOK, BACK[p][1])
+            if b:
+                pass_on(1, b, p, ts[p].at[0, 1, b], ts[p].at[1, 1, b], b)
+    for h in (0, 1):
         for p, (A, B, C) in enumerate(AXES):
             total = ts[p][0, h, 0].astype(F32)
             for o in STEPS if h else (1, 3):
@@ -429,7 +430,7 @@
         + [dma(3, 2, 4)] * 10
         + [dma(3, 4, 2), dma(3, 4, 2)],
         compiler_params=pltpu.CompilerParams(
-            collective_id=0, has_side_effects=True, vmem_limit_bytes=62_500_000
+            collective_id=0, has_side_effects=True, vmem_limit_bytes=64_000_000
         ),
         name="experts",
     )(hidden_in, routes.T, scores.T, w_gate, w_up, w_down)

time: 115 us -> 114 us (level)
    pallas_call x1, Pallas kernels: 114 us -> 113 us  [on_device(): pl.pallas_call(kernel, out_shape=pltpu.VMEM((ROWS, WIDTH), BF), in_specs=...]
where the time goes in v7:
time: 114 us; the launch traced here: 113 us
  Pallas kernels  113 us (99%)
    pallas_call x1, Pallas kernels, on_device(): pl.pallas_call(kernel, out_shape=pltpu.VMEM((ROWS, WIDTH), BF), in_specs=...  113 us

profile of v7, /device:TPU:1, one launch (start us, length us, event | category | flops | bytes accessed | tf_op | source)
XLA Modules:
  0.0 113.3 jit_solution(17800414252189632060)
XLA Ops:
  0.0 112.6 %experts.1 = bf16[32,4096]{1,0:T(8,128)(2,1)S(1)} custom-call(bf16[32,4096]{1,0:T(8,128)(2,1)} %hidden.1, s32[8,32]{1,0:T(8,128)} %bitcast.2, f32[8,32]{1,0:T(8,128)} %bitcast.3, bf16[1,4096,768]{2,1,0:T(8,128)(2,1)} %w_gate.1, bf16[1,4096,768]{2,1,0:T(8,128)(2,1)} %w_up.1, bf16[1,768,4096]{2,1,0:T(8,128)(2,1)} %w_down.1), custom_call_target="tpu_custom_call" | custom-call | tf_op jit(solution)/shard_map/experts/pallas_call | solution.py:412
  112.6 0.7 copy.8
